TPU v7x, 32 devices: a whole 2x2x4 slice. The times are simulated.
32 devices in a mesh: seq: 4 (over y, x), batch: 8 (over z, core).
Axes of the slice: x: 2, y: 2, z: 4, core: 2. Of those that a mesh axis runs over, the one named last changes fastest.
Arguments:
- byte_states: bfloat16 [2, 8, 1024, 512], P(None, 'batch', 'seq'), may hold values from -6 to 6
- teacher: bfloat16 [2, 8, 1024, 512], P(None, 'batch', 'seq'), may hold values from -96 to 96
- lengths: int32 [2, 8], P(None, 'batch'), may hold values from 256 to 1024, as said below
- conv_taps: bfloat16 [2, 9, 512], P(None, None, ('seq', 'batch')), may hold values from -2.5 to 2.5
- conv_bias: bfloat16 [2, 3, 512], P(None, None, ('seq', 'batch')), may hold values from -2.5 to 2.5
- join_weight: bfloat16 [2, 512, 512], P(None, ('seq', 'batch')), may hold values from -0.25 to 0.25
- join_bias: bfloat16 [2, 512], P(None, ('seq', 'batch')), may hold values from -2.5 to 2.5
- gain_attn: bfloat16 [2, 512], P(None, ('seq', 'batch')), may hold values from 0.5 to 1.5
- attn_in_weight: bfloat16 [2, 3, 512, 512], P(None, None, ('seq', 'batch')), may hold values from -0.125 to 0.125
- attn_out_weight: bfloat16 [2, 512, 512], P(None, ('seq', 'batch')), may hold values from -14 to 14
- position_bias: bfloat16 [2, 256], P(None, ('seq', 'batch')), may hold values from -8 to 4
- gain_mlp: bfloat16 [2, 512], P(None, ('seq', 'batch')), may hold values from 0.5 to 1.5
- mlp_in_weight: bfloat16 [2, 2, 512, 2048], P(None, None, ('seq', 'batch')), may hold values from -0.25 to 0.25
- mlp_out_weight: bfloat16 [2, 2048, 512], P(None, ('seq', 'batch')), may hold values from -0.1875 to 0.1875
Outputs:
- activations: float32 [2, 8, 1024, 512], P(None, 'batch', 'seq')
- loss: float32 [], replicated
- input_grad: float32 [2, 8, 1024, 512], P(None, 'batch', 'seq')
- grad_conv_taps: float32 [2, 9, 512], P(None, None, ('seq', 'batch'))
- grad_conv_bias: float32 [2, 3, 512], P(None, None, ('seq', 'batch'))
- grad_join_weight: float32 [2, 512, 512], P(None, ('seq', 'batch'))
- grad_join_bias: float32 [2, 512], P(None, ('seq', 'batch'))
- grad_gain_attn: float32 [2, 512], P(None, ('seq', 'batch'))
- grad_attn_in_weight: float32 [2, 3, 512, 512], P(None, None, ('seq', 'batch'))
- grad_attn_out_weight: float32 [2, 512, 512], P(None, ('seq', 'batch'))
- grad_position_bias: float32 [2, 256], P(None, ('seq', 'batch'))
- grad_gain_mlp: float32 [2, 512], P(None, ('seq', 'batch'))
- grad_mlp_in_weight: float32 [2, 2, 512, 2048], P(None, None, ('seq', 'batch'))
- grad_mlp_out_weight: float32 [2, 2048, 512], P(None, ('seq', 'batch'))
Inputs may be any that keep to these rules, and one draw needn't show every extreme that they name: `lengths`: each sequence's valid length lies between 256 and 1024; in every draw some sequence is exactly 1024 long.
All inputs are finite; a program needn't handle non-finite values.
Results may differ from a plain program's by a relative error of at most 0.017.
Values may be sent and summed in bfloat16 or wider, within the bound.
No kernel may reach another device: no remote copies, remote signals or barrier semaphores. Data moves between devices by JAX's collectives and lax.ppermute only.
A program may use at most 320 MiB of HBM per device.

v0:
```python
import jax
import jax.numpy as jnp
from jax import lax
from jax.sharding import PartitionSpec as P

HEADS = 8
HEAD_DIM = 64
BUCKETS = 32


eps = 1e-06
bounds = (12, 16, 23, 32, 46, 64, 91)
windows = ((2, 0), (3, 2), (4, 5))


def passed_along(block, axis, distance):
    devices = range(lax.axis_size(axis))
    route = [(i - distance, i) for i in devices if i - distance in devices]
    return lax.ppermute(block, axis, route)


def bucket_ids(offsets):
    magnitude = jnp.abs(offsets)
    far_ids = 8 + sum(((magnitude >= bound_value).astype(jnp.int32) for bound_value in bounds))
    near_ids = jnp.where(magnitude < 8, magnitude, far_ids)
    return jnp.where(offsets > 0, 16, 0) + near_ids


def rms_norm(values, gain):
    return values * lax.rsqrt(jnp.mean(values * values, -1, keepdims=True) + eps) * gain


def conv_sum(extended, tap_rows, biases, row_count):
    total = jnp.zeros((row_count, extended.shape[1]), jnp.float32) + jnp.sum(biases, 0)
    for window, offset in windows:
        for tap_index in range(window):
            first_row = 4 - window + tap_index
            total = (
                total + tap_rows[offset + tap_index] * extended[first_row : first_row + row_count]
            )
    return total


def project(left, right):
    return jnp.dot(left, right, preferred_element_type=jnp.float32)


def project_left(left, right):
    return lax.dot_general(
        left, right, (((0,), (0,)), ((), ())), preferred_element_type=jnp.float32
    )


def project_right(left, right):
    return lax.dot_general(
        left, right, (((1,), (1,)), ((), ())), preferred_element_type=jnp.float32
    )


def score_block(query, keys_all, pos_table, one_hot_ids, key_valid):
    query_heads = query.reshape(query.shape[0], HEADS, HEAD_DIM)
    key_heads = keys_all.reshape(keys_all.shape[0], HEADS, HEAD_DIM)
    rel_bias = jnp.einsum(
        "slb,bh->hsl",
        one_hot_ids,
        pos_table.reshape(BUCKETS, HEADS),
        preferred_element_type=jnp.float32,
    )
    scores = (
        jnp.einsum("shd,lhd->hsl", query_heads, key_heads, preferred_element_type=jnp.float32)
        + rel_bias
    )
    return jnp.where(key_valid[None, None, :], scores, -1e30)


def layer_forward(state, weights, one_hot_ids, key_valid):
    (
        tap_rows,
        biases,
        join_matrix,
        join_shift,
        gain_first,
        attn_in,
        attn_out,
        pos_table,
        gain_second,
        mlp_in,
        mlp_out,
    ) = weights
    row_count = state.shape[0]
    rounded_in = state.astype(jnp.bfloat16)
    prior_rows = passed_along(rounded_in[row_count - 3 :], "seq", 1)
    extended = jnp.concatenate([prior_rows, rounded_in], 0).astype(jnp.float32)
    mixed = conv_sum(
        extended, tap_rows.astype(jnp.float32), biases.astype(jnp.float32), row_count
    ).astype(jnp.bfloat16)
    joined = state + project(mixed, join_matrix) + join_shift.astype(jnp.float32)
    normed = rms_norm(joined, gain_first.astype(jnp.float32)).astype(jnp.bfloat16)
    projected = jnp.einsum(
        "sd,cdi->csi", normed, attn_in, preferred_element_type=jnp.float32
    ).astype(jnp.bfloat16)
    keys_all, values_all = (
        lax.all_gather(projected[1], "seq", axis=0, tiled=True),
        lax.all_gather(projected[2], "seq", axis=0, tiled=True),
    )
    scores = score_block(projected[0], keys_all, pos_table, one_hot_ids, key_valid)
    row_max = jnp.max(scores, -1, keepdims=True)
    log_total = row_max + jnp.log(jnp.sum(jnp.exp(scores - row_max), -1, keepdims=True))
    probs = jnp.exp(scores - log_total)
    value_heads = values_all.reshape(values_all.shape[0], HEADS, HEAD_DIM)
    attended = jnp.einsum(
        "hsl,lhd->shd", probs.astype(jnp.bfloat16), value_heads, preferred_element_type=jnp.float32
    )
    attended = attended.reshape(row_count, -1).astype(jnp.bfloat16)
    mid_state = joined + project(attended, attn_out)
    normed_mid = rms_norm(mid_state, gain_second.astype(jnp.float32)).astype(jnp.bfloat16)
    gate_up = jnp.einsum("sd,cdf->csf", normed_mid, mlp_in, preferred_element_type=jnp.float32)
    hidden = (jax.nn.gelu(gate_up[0], approximate=True) * gate_up[1]).astype(jnp.bfloat16)
    out_state = mid_state + project(hidden, mlp_out)
    saved = (
        extended,
        mixed,
        joined,
        normed,
        projected,
        keys_all,
        values_all,
        log_total,
        attended,
        mid_state,
        normed_mid,
        gate_up,
        hidden,
    )
    return (out_state, saved)


def gated_unit(gate_in, up_in):
    return jax.nn.gelu(gate_in, approximate=True) * up_in


def layer_backward(grad_out, saved, weights, one_hot_ids, key_valid):
    (
        tap_rows,
        biases,
        join_matrix,
        join_shift,
        gain_first,
        attn_in,
        attn_out,
        pos_table,
        gain_second,
        mlp_in,
        mlp_out,
    ) = weights
    (
        extended,
        mixed,
        joined,
        normed,
        projected,
        keys_all,
        values_all,
        log_total,
        attended,
        mid_state,
        normed_mid,
        gate_up,
        hidden,
    ) = saved
    row_count = grad_out.shape[0]
    model_width = grad_out.shape[1]
    grad_branch = grad_out.astype(jnp.bfloat16)
    grad_mlp_out = project_left(hidden, grad_branch)
    grad_hidden = project_right(grad_branch, mlp_out)
    unused_value, gelu_back = jax.vjp(gated_unit, gate_up[0], gate_up[1])
    grad_gate, grad_up = gelu_back(grad_hidden)
    grad_gate_up = jnp.stack([grad_gate, grad_up]).astype(jnp.bfloat16)
    grad_mlp_in = jnp.einsum(
        "sd,csf->cdf", normed_mid, grad_gate_up, preferred_element_type=jnp.float32
    )
    grad_normed_mid = jnp.einsum(
        "csf,cdf->sd", grad_gate_up, mlp_in, preferred_element_type=jnp.float32
    )
    unused_mid, mid_back = jax.vjp(rms_norm, mid_state, gain_second.astype(jnp.float32))
    grad_mid_part, grad_gain_second = mid_back(grad_normed_mid)
    grad_mid = grad_out + grad_mid_part
    grad_attn = grad_mid.astype(jnp.bfloat16)
    grad_attn_out = project_left(attended, grad_attn)
    grad_attended = (
        project_right(grad_attn, attn_out).astype(jnp.bfloat16).reshape(row_count, HEADS, HEAD_DIM)
    )
    query = projected[0]
    scores = score_block(query, keys_all, pos_table, one_hot_ids, key_valid)
    probs = jnp.exp(scores - log_total)
    value_heads = values_all.reshape(values_all.shape[0], HEADS, HEAD_DIM)
    key_heads = keys_all.reshape(keys_all.shape[0], HEADS, HEAD_DIM)
    query_heads = query.reshape(row_count, HEADS, HEAD_DIM)
    grad_probs = jnp.einsum(
        "shd,lhd->hsl", grad_attended, value_heads, preferred_element_type=jnp.float32
    )
    row_delta = jnp.sum(probs * grad_probs, -1, keepdims=True)
    grad_scores = (probs * (grad_probs - row_delta)).astype(jnp.bfloat16)
    grad_table = jnp.einsum(
        "slb,hsl->bh", one_hot_ids, grad_scores, preferred_element_type=jnp.float32
    ).reshape(-1)
    grad_query = jnp.einsum(
        "hsl,lhd->shd", grad_scores, key_heads, preferred_element_type=jnp.float32
    ).reshape(row_count, -1)
    grad_values_all = jnp.einsum(
        "hsl,shd->lhd",
        probs.astype(jnp.bfloat16),
        grad_attended,
        preferred_element_type=jnp.float32,
    )
    grad_keys_all = jnp.einsum(
        "hsl,shd->lhd", grad_scores, query_heads, preferred_element_type=jnp.float32
    )
    key_total = grad_keys_all.shape[0]
    grad_key, grad_value = (
        lax.psum_scatter(
            grad_keys_all.reshape(key_total, -1).astype(jnp.bfloat16),
            "seq",
            scatter_dimension=0,
            tiled=True,
        ).astype(jnp.float32),
        lax.psum_scatter(
            grad_values_all.reshape(key_total, -1).astype(jnp.bfloat16),
            "seq",
            scatter_dimension=0,
            tiled=True,
        ).astype(jnp.float32),
    )
    grad_projected = jnp.stack([grad_query, grad_key, grad_value]).astype(jnp.bfloat16)
    grad_attn_in = jnp.einsum(
        "sd,csi->cdi", normed, grad_projected, preferred_element_type=jnp.float32
    )
    grad_normed = jnp.einsum(
        "csi,cdi->sd", grad_projected, attn_in, preferred_element_type=jnp.float32
    )
    unused_joined, joined_back = jax.vjp(rms_norm, joined, gain_first.astype(jnp.float32))
    grad_joined_part, grad_gain_first = joined_back(grad_normed)
    grad_joined = grad_mid + grad_joined_part
    grad_join = grad_joined.astype(jnp.bfloat16)
    grad_join_matrix = project_left(mixed, grad_join)
    grad_join_shift = jnp.sum(grad_join.astype(jnp.float32), 0)
    grad_mixed = project_right(grad_join, join_matrix).astype(jnp.bfloat16).astype(jnp.float32)
    grad_biases = jnp.broadcast_to(jnp.sum(grad_mixed, 0), (3, model_width))
    tap_float = tap_rows.astype(jnp.float32)
    grad_taps = [None] * 9
    grad_extended = jnp.zeros((row_count + 3, model_width), jnp.float32)
    for window, offset in windows:
        for tap_index in range(window):
            first_row = 4 - window + tap_index
            grad_taps[offset + tap_index] = jnp.sum(
                grad_mixed * extended[first_row : first_row + row_count], 0
            )
            grad_extended = grad_extended + jnp.pad(
                tap_float[offset + tap_index] * grad_mixed, ((first_row, 3 - first_row), (0, 0))
            )
    back_rows = passed_along(grad_extended[:3], "seq", -1)
    grad_in = grad_joined + grad_extended[3:] + jnp.pad(back_rows, ((row_count - 3, 0), (0, 0)))
    layer_grads = (
        jnp.stack(grad_taps),
        grad_biases,
        grad_join_matrix,
        grad_join_shift,
        grad_gain_first,
        grad_attn_in,
        grad_attn_out,
        grad_table,
        grad_gain_second,
        grad_mlp_in,
        grad_mlp_out,
    )
    return (grad_in, layer_grads)


def body(
    byte_states,
    teacher,
    lengths,
    conv_taps,
    conv_bias,
    join_weight,
    join_bias,
    gain_attn,
    attn_in_weight,
    attn_out_weight,
    position_bias,
    gain_mlp,
    mlp_in_weight,
    mlp_out_weight,
):
    layer_count = conv_taps.shape[0]
    micro_count = byte_states.shape[0]
    row_count = byte_states.shape[2]
    model_width = byte_states.shape[3]
    seq_total = row_count * lax.axis_size("seq")
    positions = lax.axis_index("seq") * row_count + jnp.arange(row_count)
    key_positions = jnp.arange(seq_total)
    bucket_grid = bucket_ids(key_positions[None, :] - positions[:, None])
    one_hot_ids = (bucket_grid[:, :, None] == jnp.arange(BUCKETS)[None, None, :]).astype(
        jnp.bfloat16
    )
    total_valid = lax.psum(jnp.sum(lengths.astype(jnp.float32)), "batch")
    sums = [None] * layer_count
    out_rows = []
    grad_rows = []
    local_squares = jnp.zeros((), jnp.float32)
    for batch_index in range(micro_count):
        state = byte_states[batch_index, 0].astype(jnp.float32)
        length = lengths[batch_index, 0]
        key_valid = key_positions < length
        row_valid = positions < length
        kept = []
        for layer_index in range(layer_count):
            weights = (
                lax.all_gather(conv_taps[layer_index], ("seq", "batch"), axis=1, tiled=True),
                lax.all_gather(conv_bias[layer_index], ("seq", "batch"), axis=1, tiled=True),
                lax.all_gather(join_weight[layer_index], ("seq", "batch"), axis=0, tiled=True),
                lax.all_gather(join_bias[layer_index], ("seq", "batch"), axis=0, tiled=True),
                lax.all_gather(gain_attn[layer_index], ("seq", "batch"), axis=0, tiled=True),
                lax.all_gather(attn_in_weight[layer_index], ("seq", "batch"), axis=1, tiled=True),
                lax.all_gather(attn_out_weight[layer_index], ("seq", "batch"), axis=0, tiled=True),
                lax.all_gather(position_bias[layer_index], ("seq", "batch"), axis=0, tiled=True),
                lax.all_gather(gain_mlp[layer_index], ("seq", "batch"), axis=0, tiled=True),
                lax.all_gather(mlp_in_weight[layer_index], ("seq", "batch"), axis=1, tiled=True),
                lax.all_gather(mlp_out_weight[layer_index], ("seq", "batch"), axis=0, tiled=True),
            )
            state, saved = layer_forward(state, weights, one_hot_ids, key_valid)
            kept.append(saved)
        out_rows.append(state)
        diff = jnp.where(
            row_valid[:, None], state - teacher[batch_index, 0].astype(jnp.float32), 0.0
        )
        local_squares = local_squares + jnp.sum(diff * diff)
        grad_state = 2.0 * diff / (total_valid * model_width)
        for layer_index in reversed(range(layer_count)):
            weights = (
                lax.all_gather(conv_taps[layer_index], ("seq", "batch"), axis=1, tiled=True),
                lax.all_gather(conv_bias[layer_index], ("seq", "batch"), axis=1, tiled=True),
                lax.all_gather(join_weight[layer_index], ("seq", "batch"), axis=0, tiled=True),
                lax.all_gather(join_bias[layer_index], ("seq", "batch"), axis=0, tiled=True),
                lax.all_gather(gain_attn[layer_index], ("seq", "batch"), axis=0, tiled=True),
                lax.all_gather(attn_in_weight[layer_index], ("seq", "batch"), axis=1, tiled=True),
                lax.all_gather(attn_out_weight[layer_index], ("seq", "batch"), axis=0, tiled=True),
                lax.all_gather(position_bias[layer_index], ("seq", "batch"), axis=0, tiled=True),
                lax.all_gather(gain_mlp[layer_index], ("seq", "batch"), axis=0, tiled=True),
                lax.all_gather(mlp_in_weight[layer_index], ("seq", "batch"), axis=1, tiled=True),
                lax.all_gather(mlp_out_weight[layer_index], ("seq", "batch"), axis=0, tiled=True),
            )
            grad_state, layer_grads = layer_backward(
                grad_state, kept[layer_index], weights, one_hot_ids, key_valid
            )
            if sums[layer_index] is None:
                sums[layer_index] = layer_grads
            else:
                sums[layer_index] = jax.tree.map(jnp.add, sums[layer_index], layer_grads)
        grad_rows.append(grad_state)
    loss = lax.psum(local_squares, ("seq", "batch")) / (total_valid * model_width)
    stacked_grads = tuple(
        (
            jnp.stack([sums[layer_index][member] for layer_index in range(layer_count)])
            for member in range(11)
        )
    )
    (
        grad_taps,
        grad_biases,
        grad_join_matrix,
        grad_join_shift,
        grad_gain_first,
        grad_attn_in,
        grad_attn_out,
        grad_table,
        grad_gain_second,
        grad_mlp_in,
        grad_mlp_out,
    ) = stacked_grads
    owned = (
        lax.psum_scatter(grad_taps, ("seq", "batch"), scatter_dimension=2, tiled=True),
        lax.psum_scatter(grad_biases, ("seq", "batch"), scatter_dimension=2, tiled=True),
        lax.psum_scatter(grad_join_matrix, ("seq", "batch"), scatter_dimension=1, tiled=True),
        lax.psum_scatter(grad_join_shift, ("seq", "batch"), scatter_dimension=1, tiled=True),
        lax.psum_scatter(grad_gain_first, ("seq", "batch"), scatter_dimension=1, tiled=True),
        lax.psum_scatter(grad_attn_in, ("seq", "batch"), scatter_dimension=2, tiled=True),
        lax.psum_scatter(grad_attn_out, ("seq", "batch"), scatter_dimension=1, tiled=True),
        lax.psum_scatter(grad_table, ("seq", "batch"), scatter_dimension=1, tiled=True),
        lax.psum_scatter(grad_gain_second, ("seq", "batch"), scatter_dimension=1, tiled=True),
        lax.psum_scatter(grad_mlp_in, ("seq", "batch"), scatter_dimension=2, tiled=True),
        lax.psum_scatter(grad_mlp_out, ("seq", "batch"), scatter_dimension=1, tiled=True),
    )
    activations = jnp.stack(out_rows)[:, None]
    input_grad = jnp.stack(grad_rows)[:, None]
    return (
        activations,
        loss,
        input_grad,
        owned[0],
        owned[1],
        owned[2],
        owned[3],
        owned[4],
        owned[5],
        owned[6],
        owned[7],
        owned[8],
        owned[9],
        owned[10],
    )


def solution(mesh):
    in_specs = (
        P(None, "batch", "seq", None),
        P(None, "batch", "seq", None),
        P(None, "batch"),
        P(None, None, ("seq", "batch")),
        P(None, None, ("seq", "batch")),
        P(None, ("seq", "batch"), None),
        P(None, ("seq", "batch")),
        P(None, ("seq", "batch")),
        P(None, None, ("seq", "batch"), None),
        P(None, ("seq", "batch"), None),
        P(None, ("seq", "batch")),
        P(None, ("seq", "batch")),
        P(None, None, ("seq", "batch"), None),
        P(None, ("seq", "batch"), None),
    )
    out_specs = (
        P(None, "batch", "seq", None),
        P(),
        P(None, "batch", "seq", None),
        P(None, None, ("seq", "batch")),
        P(None, None, ("seq", "batch")),
        P(None, ("seq", "batch"), None),
        P(None, ("seq", "batch")),
        P(None, ("seq", "batch")),
        P(None, None, ("seq", "batch"), None),
        P(None, ("seq", "batch"), None),
        P(None, ("seq", "batch")),
        P(None, ("seq", "batch")),
        P(None, None, ("seq", "batch"), None),
        P(None, ("seq", "batch"), None),
    )
    return jax.shard_map(body, mesh=mesh, in_specs=in_specs, out_specs=out_specs, check_vma=False)
```

profile of v0, /device:TPU:0, one launch (start us, length us, event | category | flops | bytes accessed | tf_op | source)
XLA Modules:
  0.0 2566.9 jit_solution(86138648595676059)
XLA Ops:
  20.7 38.9 %all-gather.1 = bf16[1,9,512]{1,0,2:T(2,128)(2,1)S(1)} all-gather(bf16[1,9,16]{1,0,2:T(2,128)(2,1)S(1)} %copy.293), channel_id=3, replica_groups=mesh['seq'=4,'batch'=8] {'seq','batch'}, dimensions={2}, use_global_device_ids=true | all-gather | bytes 9504 | tf_op jit(solution)/shard_map/all_gather | solution.py:319
  60.0 37.9 %all-gather = bf16[1,3,512]{1,0,2:T(2,128)(2,1)S(1)} all-gather(bf16[1,3,16]{1,0,2:T(2,128)(2,1)S(1)} %copy.292), channel_id=2, replica_groups=mesh['seq'=4,'batch'=8] {'seq','batch'}, dimensions={2}, use_global_device_ids=true | all-gather | bytes 3168 | tf_op jit(solution)/shard_map/all_gather | solution.py:320
  102.5 40.0 %all-gather.2 = bf16[1,512,512]{2,1,0:T(8,128)(2,1)S(1)} all-gather(bf16[1,16,512]{2,1,0:T(8,128)(2,1)S(1)} %get-tuple-element.217), channel_id=4, replica_groups=mesh['seq'=4,'batch'=8] {'seq','batch'}, dimensions={1}, use_global_device_ids=true | all-gather | bytes 540672 | tf_op jit(solution)/shard_map/all_gather | solution.py:321
  142.5 15.7 slice_reduce_fusion.17
  161.2 41.4 %all-reduce.53 = (bf16[512]{0:T(512)(128)(2,1)S(1)}, bf16[512]{0:T(512)(128)(2,1)S(1)}, bf16[256]{0:T(256)(128)(2,1)}, bf16[512]{0:T(512)(128)(2,1)}, bf16[512]{...) all-reduce(bf16[512]{0:T(512)(128)(2,1)S(1)} %dynamic-update-slice,, ...), channel_id=5, replica_groups=mesh['seq'=4,'batch'=8] {'seq','batch'}, use_global_device_ids=true, to_apply=%add.40 | all-reduce | flops 3584 | bytes 14336
  218.3 8.0 iota_compare_fusion
  226.4 46.1 %copy.214 = pred[256,1024,32]{1,2,0:T(32,128)(4,1)} copy(pred[256,1024,32]{0,2,1:T(32,128)(4,1)} %iota_compare_fusion) | data formatting | bytes 16777216 | tf_op jit(solution)/shard_map/eq | solution.py:303
  273.7 43.5 %all-gather.9 = bf16[1,512,512]{2,1,0:T(8,128)(2,1)S(1)} all-gather(bf16[1,16,512]{2,1,0:T(8,128)(2,1)S(1)} %get-tuple-element.215), channel_id=11, replica_groups=mesh['seq'=4,'batch'=8] {'seq','batch'}, dimensions={1}, use_global_device_ids=true | all-gather | bytes 540672 | tf_op jit(solution)/shard_map/all_gather | solution.py:325
  318.0 38.1 %all-gather.14 = bf16[1,9,512]{1,0,2:T(2,128)(2,1)S(1)} all-gather(bf16[1,9,16]{1,0,2:T(2,128)(2,1)S(1)} %copy.295), channel_id=16, replica_groups=mesh['seq'=4,'batch'=8] {'seq','batch'}, dimensions={2}, use_global_device_ids=true | all-gather | bytes 9504 | tf_op jit(solution)/shard_map/all_gather | solution.py:319
  356.3 15.7 slice_reduce_fusion.8
  372.2 39.1 %all-gather.13 = bf16[1,3,512]{1,0,2:T(2,128)(2,1)S(1)} all-gather(bf16[1,3,16]{1,0,2:T(2,128)(2,1)S(1)} %copy.294), channel_id=15, replica_groups=mesh['seq'=4,'batch'=8] {'seq','batch'}, dimensions={2}, use_global_device_ids=true | all-gather | bytes 3168 | tf_op jit(solution)/shard_map/all_gather | solution.py:320
  412.3 40.1 %all-gather.15 = bf16[1,512,512]{2,1,0:T(8,128)(2,1)S(1)} all-gather(bf16[1,16,512]{2,1,0:T(8,128)(2,1)S(1)} %copy-done.157), channel_id=17, replica_groups=mesh['seq'=4,'batch'=8] {'seq','batch'}, dimensions={1}, use_global_device_ids=true | all-gather | bytes 540672 | tf_op jit(solution)/shard_map/all_gather | solution.py:321
  452.4 8.5 fusion.279
  463.6 9.6 fusion.349
  487.3 9.9 fusion.350
  546.0 8.3 fusion.277
  554.4 41.1 %all-gather.22 = bf16[1,512,512]{2,1,0:T(8,128)(2,1)S(1)} all-gather(bf16[1,16,512]{2,1,0:T(8,128)(2,1)S(1)} %get-tuple-element.214), channel_id=24, replica_groups=mesh['seq'=4,'batch'=8] {'seq','batch'}, dimensions={1}, use_global_device_ids=true | all-gather | bytes 540672 | tf_op jit(solution)/shard_map/all_gather | solution.py:325
  595.5 14.8 psum.15
  614.5 9.6 fusion.354
  629.8 5.9 convolution_convert_fusion.22
  638.2 13.1 fusion.353
  664.1 49.5 %all-gather.61.cloned.1.call-done = bf16[1,2,512,2048]{3,2,1,0:T(8,128)(2,1)} async-done(((bf16[1,2,16,2048]{3,2,1,0:T(8,128)(2,1)}), bf16[1,2,512,2048]{3,2,1,0:T(8,128)(2,1)}) %all-gather.61.cloned.1.call-update) | async-done | bytes 4194320 | tf_op jit(solution)/shard_map/all_gather | solution.py:328
  722.9 49.2 %all-gather.63.cloned.1.call-done = bf16[1,2048,512]{2,1,0:T(8,128)(2,1)} async-done(((bf16[1,64,512]{2,1,0:T(8,128)(2,1)}), bf16[1,2048,512]{2,1,0:T(8,128)(2,1)}) %all-gather.63.cloned.1.call-update) | async-done | bytes 2097168 | tf_op jit(solution)/shard_map/all_gather | solution.py:329
  792.6 6.2 multiply_reduce_fusion.3
  806.7 6.0 convolution_convert_fusion.6
  832.8 5.9 convolution_convert_fusion.2
  867.5 27.6 %reduce-scatter.36.cloned.1.call-done = bf16[256,512]{1,0:T(8,128)(2,1)} async-done(((bf16[1024,512]{1,0:T(8,128)(2,1)}), bf16[256,512]{1,0:T(8,128)(2,1)}) %reduce-scatter.36.cloned.1.call-update) | async-done | bytes 262160 | tf_op jit(solution)/shard_map/reduce_scatter | solution.py:221
  895.1 30.7 %reduce-scatter.38.cloned.1.call-done = bf16[256,512]{1,0:T(8,128)(2,1)} async-done(((bf16[1024,512]{1,0:T(8,128)(2,1)}), bf16[256,512]{1,0:T(8,128)(2,1)}) %reduce-scatter.38.cloned.1.call-update) | async-done | bytes 262160 | tf_op jit(solution)/shard_map/reduce_scatter | solution.py:227
  1000.2 6.3 fusion.116
  1012.7 10.1 pad_maximum_fusion
  1022.7 25.6 copy.263
  1059.7 24.1 reduce-scatter.42.cloned.1.call-done
  1113.5 10.4 copy.252
  1144.0 7.0 copy.256
  1151.0 7.0 copy.257
  1158.0 7.1 fusion.170
  1172.1 7.0 copy.254
  1179.0 7.0 copy.253
  1186.0 7.1 fusion.171
  1200.1 39.3 %all-reduce.51 = (f32[]{:T(128)}, f32[2,256]{1,0:T(2,128)S(1)}) all-reduce(f32[]{:T(128)S(6)} %add.965, f32[2,256]{1,0:T(2,128)S(1)} %pad_maximum_fusion.42), channel_id=1, replica_groups=mesh['seq'=4,'batch'=8] {'seq','batch'}, use_global_device_ids=true, to_apply=%region_20.21 | all-reduce | flops 513 | bytes 4104 | tf_op jit(solution)/shard_map/psum | solution.py:361
  1254.7 100.7 %reduce-scatter.56.cloned.1.call-done = f32[16,2]{1,0:T(8,128)} async-done(((f32[512,2]{1,0:T(8,128)}), f32[16,2]{1,0:T(8,128)}) %reduce-scatter.56.cloned.1.call-update) | async-done | bytes 144
  1356.8 132.9 %reduce-scatter.54.cloned.1.call-done = f32[16,2]{1,0:T(8,128)} async-done(((f32[512,2]{1,0:T(8,128)}), f32[16,2]{1,0:T(8,128)}) %reduce-scatter.54.cloned.1.call-update) | async-done | bytes 144
  1491.0 132.7 %reduce-scatter.52.cloned.1.call-done = f32[16,6]{1,0:T(8,128)} async-done(((f32[512,6]{1,0:T(8,128)}), f32[16,6]{1,0:T(8,128)}) %reduce-scatter.52.cloned.1.call-update) | async-done | bytes 400
  1625.1 132.6 %reduce-scatter.50.cloned.1.call-done = f32[16,18]{1,0:T(8,128)} async-done(((f32[512,18]{1,0:T(8,128)}), f32[16,18]{1,0:T(8,128)}) %reduce-scatter.50.cloned.1.call-update) | async-done | bytes 1168
  1759.2 368.1 %all-reduce.56.cloned.1.call-done = (f32[2,3,512,512]{3,0,1,2:T(2,128)}, f32[2,2,512,2048]{3,1,0,2:T(2,128)}) async-done(((f32[2,3,512,512]{3,0,1,2:T(2,128)}, f32[2,2,512,2048]{3,1,0,2:T(2,128)}), (f32[2,3,512,512]{3,0,1,2:T(2,128)}, f32[2,2,512,2048]{3,1,0,2:T(2,128)})) %all-reduce.56.cloned.1.call-update) | async-done | bytes 23068688
  2131.2 136.6 %reduce-scatter.46.cloned.1.call-done = f32[2,16,512]{2,1,0:T(8,128)} async-done(((f32[2,512,512]{2,1,0:T(8,128)}), f32[2,16,512]{2,1,0:T(8,128)}) %reduce-scatter.46.cloned.1.call-update) | async-done | bytes 65552 | tf_op jit(solution)/shard_map/reduce_scatter | solution.py:388
  2267.8 137.3 %reduce-scatter.44.cloned.1.call-done = f32[2,16,512]{2,1,0:T(8,128)} async-done(((f32[2,512,512]{2,1,0:T(8,128)}), f32[2,16,512]{2,1,0:T(8,128)}) %reduce-scatter.44.cloned.1.call-update) | async-done | bytes 65552 | tf_op jit(solution)/shard_map/reduce_scatter | solution.py:384
  2405.1 153.6 %reduce-scatter.48.cloned.1.call-done = f32[2,64,512]{2,1,0:T(8,128)} async-done(((f32[2,2048,512]{2,1,0:T(8,128)}), f32[2,64,512]{2,1,0:T(8,128)}) %reduce-scatter.48.cloned.1.call-update) | async-done | bytes 262160 | tf_op jit(solution)/shard_map/reduce_scatter | solution.py:392
  (850 shorter events, 391.9 us)
Async XLA Ops:
  7.2 197.9 %all-gather.45.cloned.1.call-start = ((), (), s32[]{:S(2)}) async-start(), calls=%async_computation.27 | async-start | bytes 1622016 | tf_op jit(solution)/shard_map/all_gather | solution.py:324
  8.0 194.6 %collective-permute-start = (bf16[3,512]{1,0:T(4,128)(2,1)S(1)}, bf16[3,512]{1,0:T(4,128)(2,1)S(1)}, u32[]{:S(2)}, u32[]{:S(2)}) collective-permute-start(bf16[3,512]{1,0:T(4,128)(2,1)S(1)} %get-tuple-element.168), channel_id=1, source_target_pairs={{0,8},{8,16},{16,24},{1,9},{9,17},{17,25},{2,10},{10,18},{18,26},{... | collective-permute-start | bytes 9224 | tf_op jit(solution)/shard_map/ppermute | solution.py:19
  12.8 189.9 %collective-permute-start.2 = (bf16[3,512]{1,0:T(4,128)(2,1)S(1)}, bf16[3,512]{1,0:T(4,128)(2,1)S(1)}, u32[]{:S(2)}, u32[]{:S(2)}) collective-permute-start(bf16[3,512]{1,0:T(4,128)(2,1)S(1)} %get-tuple-element.169), channel_id=1, source_target_pairs={{0,8},{8,16},{16,24},{1,9},{9,17},{17,25},{2,10},{10,18},{18,26},{... | collective-permute-start | bytes 9224 | tf_op jit(solution)/shard_map/ppermute | solution.py:19
  17.7 443.5 %all-gather.67.cloned.1.call-start = ((), (), s32[]{:S(2)}) async-start(), calls=%async_computation.38 | async-start | bytes 1310720 | tf_op jit(solution)/shard_map/all_gather | solution.py:103
  205.0 279.2 %copy-start.37 = (f32[256,512]{1,0:T(8,128)}, f32[256,512]{1,0:T(8,128)S(1)}, u32[]{:S(2)}) copy-start(f32[256,512]{1,0:T(8,128)S(1)} %get-tuple-element.251) | copy-start | bytes 1572868
  208.3 268.4 %all-gather.65.cloned.1.call-start = ((), (), s32[]{:S(2)}) async-start(), calls=%async_computation.37 | async-start | bytes 1310720 | tf_op jit(solution)/shard_map/all_gather | solution.py:104
  209.0 275.6 %all-gather.49.cloned.1.call-start = ((), (), s32[]{:S(2)}) async-start(), calls=%async_computation.29 | async-start | bytes 1310720 | tf_op jit(solution)/shard_map/all_gather | solution.py:103
  210.5 297.5 %copy-start.39 = (f32[256,512]{1,0:T(8,128)}, f32[256,512]{1,0:T(8,128)S(1)}, u32[]{:S(2)}) copy-start(f32[256,512]{1,0:T(8,128)S(1)} %get-tuple-element.257) | copy-start | bytes 1572868
  212.6 287.9 %all-gather.47.cloned.1.call-start = ((), (), s32[]{:S(2)}) async-start(), calls=%async_computation.28 | async-start | bytes 1310720 | tf_op jit(solution)/shard_map/all_gather | solution.py:104
  213.2 295.5 %all-gather.51.cloned.1.call-start = ((), (), s32[]{:S(2)}) async-start(), calls=%async_computation.30 | async-start | bytes 4325376 | tf_op jit(solution)/shard_map/all_gather | solution.py:328
  214.9 300.2 %all-gather.53.cloned.1.call-start = ((), (), s32[]{:S(2)}) async-start(), calls=%async_computation.31 | async-start | bytes 2162688 | tf_op jit(solution)/shard_map/all_gather | solution.py:329
  215.7 316.7 %all-gather.55.cloned.1.call-start = ((), (), s32[]{:S(2)}) async-start(), calls=%async_computation.32 | async-start | bytes 1622016 | tf_op jit(solution)/shard_map/all_gather | solution.py:324
  216.4 395.8 %all-gather.59.cloned.1.call-start = ((), (), s32[]{:S(2)}) async-start(), calls=%async_computation.34 | async-start | bytes 1310720 | tf_op jit(solution)/shard_map/all_gather | solution.py:103
  226.4 90.8 %copy-start.215 = (bf16[512]{0:T(512)(128)(2,1)S(1)}, bf16[512]{0:T(512)(128)(2,1)}, u32[]{:S(2)}) copy-start(bf16[512]{0:T(512)(128)(2,1)} %get-tuple-element.133) | copy-start | bytes 3076
  226.4 145.7 %copy-start.201 = (bf16[1,3,16]{2,0,1:T(2,128)(2,1)S(1)}, bf16[1,3,16]{2,0,1:T(2,128)(2,1)}, u32[]{:S(2)}) copy-start(bf16[1,3,16]{2,0,1:T(2,128)(2,1)} %get-tuple-element.238) | copy-start | bytes 292
  272.5 139.8 %copy-start.214 = (bf16[512]{0:T(512)(128)(2,1)S(1)}, bf16[512]{0:T(512)(128)(2,1)}, u32[]{:S(2)}) copy-start(bf16[512]{0:T(512)(128)(2,1)} %get-tuple-element.134) | copy-start | bytes 3076
  272.5 139.8 %copy-start.157 = (bf16[1,16,512]{2,1,0:T(8,128)(2,1)S(1)}, bf16[1,16,512]{2,1,0:T(8,128)(2,1)}, u32[]{:S(2)}) copy-start(bf16[1,16,512]{2,1,0:T(8,128)(2,1)} %get-tuple-element.216) | copy-start | bytes 49156
  272.5 179.9 %copy-start.213 = (bf16[512]{0:T(512)(128)(2,1)S(1)}, bf16[512]{0:T(512)(128)(2,1)}, u32[]{:S(2)}) copy-start(bf16[512]{0:T(512)(128)(2,1)} %get-tuple-element.135) | copy-start | bytes 3076
  452.4 79.3 %copy-start.50 = (bf16[1,512,512]{2,1,0:T(8,128)(2,1)}, bf16[1,512,512]{2,1,0:T(8,128)(2,1)S(1)}, u32[]{:S(2)}) copy-start(bf16[1,512,512]{2,1,0:T(8,128)(2,1)S(1)} %all-gather.15) | copy-start | bytes 1572868
  518.7 10.8 collective-permute-start.3
  525.3 5.4 collective-permute-start.1
  535.6 91.9 %all-gather.57.cloned.1.call-start = ((), (), s32[]{:S(2)}) async-start(), calls=%async_computation.33 | async-start | bytes 1310720 | tf_op jit(solution)/shard_map/all_gather | solution.py:104
  536.2 99.5 %all-gather.71.cloned.1.call-start = ((), (), s32[]{:S(2)}) async-start(), calls=%async_computation.40 | async-start | bytes 1310720 | tf_op jit(solution)/shard_map/all_gather | solution.py:103
  541.0 110.3 %all-gather.69.cloned.1.call-start = ((), (), s32[]{:S(2)}) async-start(), calls=%async_computation.39 | async-start | bytes 1310720 | tf_op jit(solution)/shard_map/all_gather | solution.py:104
  541.6 172.0 %all-gather.61.cloned.1.call-start = ((), (), s32[]{:S(2)}) async-start(), calls=%async_computation.35 | async-start | bytes 4325376 | tf_op jit(solution)/shard_map/all_gather | solution.py:328
  542.3 229.7 %all-gather.63.cloned.1.call-start = ((), (), s32[]{:S(2)}) async-start(), calls=%async_computation.36 | async-start | bytes 2162688 | tf_op jit(solution)/shard_map/all_gather | solution.py:329
  542.9 315.8 %reduce-scatter.28.cloned.1.call-start = ((), (), s32[]{:S(2)}) async-start(), calls=%async_computation.16 | async-start | bytes 1310720 | tf_op jit(solution)/shard_map/reduce_scatter | solution.py:221
  806.7 57.7 %reduce-scatter.30.cloned.1.call-start = ((), (), s32[]{:S(2)}) async-start(), calls=%async_computation.17 | async-start | bytes 1310720 | tf_op jit(solution)/shard_map/reduce_scatter | solution.py:227
  815.0 80.1 %reduce-scatter.36.cloned.1.call-start = ((), (), s32[]{:S(2)}) async-start(), calls=%async_computation.20 | async-start | bytes 1310720 | tf_op jit(solution)/shard_map/reduce_scatter | solution.py:221
  832.6 93.2 %reduce-scatter.38.cloned.1.call-start = ((), (), s32[]{:S(2)}) async-start(), calls=%async_computation.21 | async-start | bytes 1310720 | tf_op jit(solution)/shard_map/reduce_scatter | solution.py:227
  841.1 215.2 %reduce-scatter.34.cloned.1.call-start = ((), (), s32[]{:S(2)}) async-start(), calls=%async_computation.19 | async-start | bytes 1310720 | tf_op jit(solution)/shard_map/reduce_scatter | solution.py:227
  845.4 80.4 %copy-start.137 = (bf16[1,256,512]{2,1,0:T(8,128)(2,1)}, bf16[1,256,512]{2,1,0:T(8,128)(2,1)S(1)}, u32[]{:S(2)}) copy-start(bf16[1,256,512]{2,1,0:T(8,128)(2,1)S(1)} %copy.243) | copy-start | bytes 786436
  932.2 5.5 collective-permute-start.6
  935.0 6.4 collective-permute-start.4
  961.2 95.2 %reduce-scatter.32.cloned.1.call-start = ((), (), s32[]{:S(2)}) async-start(), calls=%async_computation.18 | async-start | bytes 1310720 | tf_op jit(solution)/shard_map/reduce_scatter | solution.py:221
  975.5 84.3 %reduce-scatter.40.cloned.1.call-start = ((), (), s32[]{:S(2)}) async-start(), calls=%async_computation.22 | async-start | bytes 1310720 | tf_op jit(solution)/shard_map/reduce_scatter | solution.py:221
  990.6 93.3 %reduce-scatter.42.cloned.1.call-start = ((), (), s32[]{:S(2)}) async-start(), calls=%async_computation.23 | async-start | bytes 1310720 | tf_op jit(solution)/shard_map/reduce_scatter | solution.py:227
  1000.2 240.5 %reduce-scatter.58.cloned.1.call-start = ((), (), s32[]{:S(2)}) async-start(), calls=%async_computation.45 | async-start | bytes 270336
  1056.1 299.4 %reduce-scatter.56.cloned.1.call-start = ((), (), s32[]{:S(2)}) async-start(), calls=%async_computation.44 | async-start | bytes 270336
  1097.7 391.9 %reduce-scatter.54.cloned.1.call-start = ((), (), s32[]{:S(2)}) async-start(), calls=%async_computation.43 | async-start | bytes 270336
  1098.7 525.0 %reduce-scatter.52.cloned.1.call-start = ((), (), s32[]{:S(2)}) async-start(), calls=%async_computation.42 | async-start | bytes 270336
  1100.4 657.4 %reduce-scatter.50.cloned.1.call-start = ((), (), s32[]{:S(2)}) async-start(), calls=%async_computation.41 | async-start | bytes 270336
  1107.8 1019.5 %all-reduce.56.cloned.1.call-start = ((), (), s32[]{:S(2)}) async-start(), calls=%async_computation.46 | async-start | bytes 46137344
  1124.0 1143.8 %reduce-scatter.46.cloned.1.call-start = ((), (), s32[]{:S(2)}) async-start(), calls=%async_computation.25 | async-start | bytes 2162688 | tf_op jit(solution)/shard_map/reduce_scatter | solution.py:388
  1127.8 1277.3 %reduce-scatter.44.cloned.1.call-start = ((), (), s32[]{:S(2)}) async-start(), calls=%async_computation.24 | async-start | bytes 2162688 | tf_op jit(solution)/shard_map/reduce_scatter | solution.py:384
  1134.0 1424.7 %reduce-scatter.48.cloned.1.call-start = ((), (), s32[]{:S(2)}) async-start(), calls=%async_computation.26 | async-start | bytes 8650752 | tf_op jit(solution)/shard_map/reduce_scatter | solution.py:392
  1245.0 5.9 collective-permute-start.5
  1247.2 6.4 collective-permute-start.7
  (216 other events, 2587.7 us)
Sparse Core Ops, SparseCore 0:
  17.8 55.4 all-gather.44
  208.4 27.1 all-gather.66
  238.0 26.4 all-gather.64
  266.3 27.3 all-gather.48
  295.3 26.3 all-gather.46
  324.7 62.0 all-gather.50
  390.3 55.2 all-gather.52
  448.7 54.2 all-gather.54
  535.7 26.1 all-gather.58
  563.6 27.8 all-gather.56
  593.9 26.0 all-gather.70
  621.8 26.4 all-gather.68
  651.9 61.6 all-gather.60
  717.0 55.0 all-gather.62
  806.8 26.7 reduce-scatter.27
  836.4 27.9 reduce-scatter.29
  867.1 27.9 reduce-scatter.35
  897.8 27.9 reduce-scatter.37
  961.3 29.4 reduce-scatter.33
  993.5 27.9 reduce-scatter.31
  1024.4 27.9 reduce-scatter.39
  1055.9 27.9 reduce-scatter.41
  1086.1 135.3 reduce-scatter.57
  1223.5 131.8 reduce-scatter.55
  1357.7 131.9 reduce-scatter.53
  1491.7 131.9 reduce-scatter.51
  1625.8 131.9 reduce-scatter.49
  1764.2 363.1 all-reduce.55
  2130.2 137.5 reduce-scatter.45
  2270.4 134.6 reduce-scatter.43
  2408.0 150.7 reduce-scatter.47
where the time goes:
time: 2580 us; the launch traced here: 2570 us
  waiting for transfers between devices  1500 us (58%)
  blocking collectives  414 us (16%)
  matrix products  280 us (11%)
  local copies, waits for them, and re-layouts  258 us (10%)
  other arithmetic  74.1 us (3%)
    unnamed x37, waiting for transfers between devices  872 us
    reduce_scatter x1, waiting for transfers between devices, body(): lax.psum_scatter(grad_mlp_out, ('seq', 'batch'), scatter_dimension=1, til...  154 us
    reduce_scatter x1, waiting for transfers between devices, body(): lax.psum_scatter(grad_join_matrix, ('seq', 'batch'), scatter_dimension=1,...  137 us
    reduce_scatter x1, waiting for transfers between devices, body(): lax.psum_scatter(grad_attn_out, ('seq', 'batch'), scatter_dimension=1, ti...  137 us
    all_gather x2, blocking collectives, body(): lax.all_gather(attn_out_weight[layer_index], ('seq', 'batch'), axis=0, ti...  84.6 us
    all_gather x2, blocking collectives, body(): lax.all_gather(join_weight[layer_index], ('seq', 'batch'), axis=0, tiled=...  80.1 us
    all_gather x2, blocking collectives, body(): lax.all_gather(conv_taps[layer_index], ('seq', 'batch'), axis=1, tiled=True)  77 us
    all_gather x2, blocking collectives, body(): lax.all_gather(conv_bias[layer_index], ('seq', 'batch'), axis=1, tiled=True)  77 us
  transfers between devices with their start and end apart: 39, of which 19 were waited for; matrix products, arithmetic and copies ran while one was open for 20% of the time, Pallas kernels for 0%

commit v1 on v0

--- a/solution.py
+++ b/solution.py
@@ -1,6 +1,9 @@
 import jax
 import jax.numpy as jnp
 from jax import lax
+from jax.experimental import pallas as pl
+from jax.experimental.pallas import tpu as pltpu
+from jax.sharding import Mesh
 from jax.sharding import PartitionSpec as P
 
 HEADS = 8
@@ -411,7 +414,606 @@
     )
 
 
-def solution(mesh):
+ALL = ("seq", "z", "core")
+LOW = jnp.bfloat16
+WIDE = jnp.float32
+BLOCK = 256
+MASKED = -1e30
+
+
+def nt(left, right):
+    return lax.dot_general(left, right, (((1,), (1,)), ((), ())), preferred_element_type=WIDE)
+
+
+def nn(left, right):
+    return lax.dot_general(left, right, (((1,), (0,)), ((), ())), preferred_element_type=WIDE)
+
+
+def tn(left, right):
+    return lax.dot_general(left, right, (((0,), (0,)), ((), ())), preferred_element_type=WIDE)
+
+
+def band_kernel(line_ref, band_ref):
+    wide = jnp.broadcast_to(line_ref[0], (BLOCK, 4 * BLOCK))
+    rolled = pltpu.roll(wide, 0, 1, stride=1, stride_axis=0)
+    band_ref[0, 0] = rolled[:, :BLOCK]
+    band_ref[0, 1] = rolled[:, BLOCK : 2 * BLOCK]
+    band_ref[0, 2] = rolled[:, 3 * BLOCK :]
+
+
+def build_band(line):
+    return pl.pallas_call(
+        band_kernel,
+        grid=(HEADS,),
+        in_specs=[pl.BlockSpec((1, 1, 4 * BLOCK), lambda h: (h, 0, 0))],
+        out_specs=pl.BlockSpec((1, 3, BLOCK, BLOCK), lambda h: (h, 0, 0, 0)),
+        out_shape=jax.ShapeDtypeStruct((HEADS, 3, BLOCK, BLOCK), WIDE),
+        name="bias_band",
+    )(line.reshape(HEADS, 1, 4 * BLOCK))
+
+
+def key_blocks(core, near):
+    near_rows = pl.multiple_of(BLOCK * (1 - core), BLOCK)
+    far_rows = pl.multiple_of(BLOCK * core, BLOCK)
+    below, above = 1 + core, 2 - core
+    if near:
+        return near_rows, ((0, near_rows, 0), (0, far_rows, below), (1, far_rows, above), (1, near_rows, None))
+    return far_rows, ((0, far_rows, 0), (0, near_rows, above), (1, far_rows, None), (1, near_rows, None))
+
+
+def keys_with_mask(block, lane, head, first_position, length, constant):
+    rows = first_position + lax.broadcasted_iota(jnp.int32, (BLOCK, 1), 0)
+    mask = jnp.where(rows < length, 0.0, MASKED)
+    spare = (1 - head) * HEAD_DIM
+    extra = jnp.where(lane == spare, mask, jnp.where(lane == spare + 1, constant, 0.0))
+    return jnp.where(lane // HEAD_DIM == head, block.astype(WIDE), extra).astype(LOW)
+
+
+def query_with_ones(block, lane, head):
+    spare = (1 - head) * HEAD_DIM
+    extra = jnp.where((lane == spare) | (lane == spare + 1), 1.0, 0.0)
+    return jnp.where(lane // HEAD_DIM == head, block.astype(WIDE), extra).astype(LOW)
+
+
+def only_head(block, lane, head):
+    return jnp.where(lane // HEAD_DIM == head, block.astype(WIDE), 0.0).astype(LOW)
+
+
+def attend_kernel(
+    info_ref, far_ref, q_ref, k_ref, v_ref, ko_ref, vo_ref, band_ref, out_ref, lse_ref, score_ref
+):
+    core, length = info_ref[0], info_ref[1]
+    pair = pl.program_id(0)
+    lane = lax.broadcasted_iota(jnp.int32, (1, 2 * HEAD_DIM), 1)
+    for n in range(2):
+        q_rows, blocks = key_blocks(core, n == 0)
+        query = q_ref[pl.ds(q_rows, BLOCK), :]
+        halves = []
+        for head in range(2):
+            q_low = query_with_ones(query, lane, head)
+            top = None
+            for b, (side, start, slot) in enumerate(blocks):
+                first = 2 * BLOCK * (core if side == 0 else 1 - core) + start
+                keys = (k_ref, ko_ref)[side][pl.ds(start, BLOCK), :]
+                constant = far_ref[2 * pair + head] if slot is None else 0.0
+                scores = nt(keys_with_mask(keys, lane, head, first, length, constant), q_low)
+                if slot is not None:
+                    scores = scores + band_ref[head, slot]
+                score_ref[b] = scores
+                block_top = jnp.max(scores, 0, keepdims=True)
+                top = block_top if top is None else jnp.maximum(top, block_top)
+            total = jnp.zeros((1, BLOCK), WIDE)
+            mixed = jnp.zeros((2 * HEAD_DIM, BLOCK), WIDE)
+            for b, (side, start, slot) in enumerate(blocks):
+                weights = jnp.exp(score_ref[b] - top)
+                total = total + jnp.sum(weights, 0, keepdims=True)
+                values = (v_ref, vo_ref)[side][pl.ds(start, BLOCK), :]
+                mixed = mixed + tn(values, weights.astype(LOW))
+            lse_ref[0, n, head : head + 1, :] = top + jnp.log(total)
+            halves.append((mixed / total)[head * HEAD_DIM : (head + 1) * HEAD_DIM])
+        out_ref[pl.ds(q_rows, BLOCK), :] = jnp.transpose(jnp.concatenate(halves, 0)).astype(LOW)
+
+
+def attend(info, far, projected, others, band):
+    rows = projected.shape[0]
+    pairs = HEADS // 2
+    width = 2 * HEAD_DIM
+    col = lambda shift: pl.BlockSpec((rows, width), lambda p: (0, p + shift))
+    return pl.pallas_call(
+        attend_kernel,
+        grid=(pairs,),
+        in_specs=[
+            pl.BlockSpec(memory_space=pltpu.SMEM),
+            pl.BlockSpec(memory_space=pltpu.SMEM),
+            col(0),
+            col(pairs),
+            col(2 * pairs),
+            col(0),
+            col(pairs),
+            pl.BlockSpec((2, 3, BLOCK, BLOCK), lambda p: (p, 0, 0, 0)),
+        ],
+        out_specs=[col(0), pl.BlockSpec((1, 2, 2, BLOCK), lambda p: (p, 0, 0, 0))],
+        out_shape=[
+            jax.ShapeDtypeStruct((rows, HEADS * HEAD_DIM), LOW),
+            jax.ShapeDtypeStruct((pairs, 2, 2, BLOCK), WIDE),
+        ],
+        scratch_shapes=[pltpu.VMEM((4, BLOCK, BLOCK), WIDE)],
+        name="attend",
+    )(info, far, projected, projected, projected, others, others, band)
+
+
+def attend_back_kernel(
+    info_ref,
+    far_ref,
+    q_ref,
+    k_ref,
+    v_ref,
+    ko_ref,
+    vo_ref,
+    band_ref,
+    out_ref,
+    gout_ref,
+    lse_ref,
+    gq_ref,
+    gown_ref,
+    goth_ref,
+    gband_ref,
+    gfar_ref,
+    gk_acc,
+    gv_acc,
+    band_acc,
+    far_acc,
+):
+    core, length = info_ref[0], info_ref[1]
+    pair = pl.program_id(0)
+    width = 2 * HEAD_DIM
+    lane = lax.broadcasted_iota(jnp.int32, (1, width), 1)
+    gk_acc[...] = jnp.zeros_like(gk_acc)
+    gv_acc[...] = jnp.zeros_like(gv_acc)
+    band_acc[...] = jnp.zeros_like(band_acc)
+    far_acc[...] = jnp.zeros_like(far_acc)
+    select = jnp.where(
+        lax.broadcasted_iota(jnp.int32, (8, width), 0)
+        == lax.broadcasted_iota(jnp.int32, (8, width), 1) // HEAD_DIM,
+        1.0,
+        0.0,
+    )
+    for n in range(2):
+        q_rows, blocks = key_blocks(core, n == 0)
+        query = q_ref[pl.ds(q_rows, BLOCK), :]
+        gout = gout_ref[pl.ds(q_rows, BLOCK), :]
+        dots = gout.astype(WIDE) * out_ref[pl.ds(q_rows, BLOCK), :].astype(WIDE)
+        deltas = lax.dot_general(
+            select,
+            dots,
+            (((1,), (1,)), ((), ())),
+            precision=lax.Precision.HIGHEST,
+            preferred_element_type=WIDE,
+        )
+        halves = []
+        for head in range(2):
+            q_ones = query_with_ones(query, lane, head)
+            q_low = only_head(query, lane, head)
+            g_low = only_head(gout, lane, head)
+            lse = lse_ref[0, n, head : head + 1, :]
+            delta = deltas[head : head + 1]
+            gq = jnp.zeros((width, BLOCK), WIDE)
+            for side, start, slot in blocks:
+                first = 2 * BLOCK * (core if side == 0 else 1 - core) + start
+                keys = (k_ref, ko_ref)[side][pl.ds(start, BLOCK), :]
+                values = (v_ref, vo_ref)[side][pl.ds(start, BLOCK), :]
+                constant = far_ref[2 * pair + head] if slot is None else 0.0
+                scores = nt(keys_with_mask(keys, lane, head, first, length, constant), q_ones)
+                if slot is not None:
+                    scores = scores + band_ref[head, slot]
+                probs = jnp.exp(scores - lse)
+                gprobs = nt(values, g_low)
+                gscores = probs * (gprobs - delta)
+                if slot is None:
+                    part = jnp.sum(gscores.reshape(BLOCK // 8, 8, BLOCK), 0)
+                    far_acc[head] = far_acc[head] + part
+                else:
+                    band_acc[head, slot] = band_acc[head, slot] + gscores
+                gs_low = gscores.astype(LOW)
+                at = pl.ds(2 * BLOCK * side + start, BLOCK)
+                gv_acc[at, :] = gv_acc[at, :] + nn(probs.astype(LOW), g_low)
+                gk_acc[at, :] = gk_acc[at, :] + nn(gs_low, q_low)
+                gq = gq + tn(keys, gs_low)
+            halves.append(gq[head * HEAD_DIM : (head + 1) * HEAD_DIM])
+        gq_ref[pl.ds(q_rows, BLOCK), :] = jnp.transpose(jnp.concatenate(halves, 0)).astype(LOW)
+    own = 2 * BLOCK
+    gown_ref[0] = gk_acc[:own, :]
+    gown_ref[1] = gv_acc[:own, :]
+    goth_ref[0] = gk_acc[own:, :].astype(LOW)
+    goth_ref[1] = gv_acc[own:, :].astype(LOW)
+    span = 4 * BLOCK
+    gap = jnp.zeros((8, BLOCK), WIDE)
+    row = lax.broadcasted_iota(jnp.int32, (8, span), 0)
+    for head in range(2):
+        lines = jnp.zeros((8, span), WIDE)
+        for g in range(BLOCK // 8):
+            rows = slice(8 * g, 8 * g + 8)
+            piece = jnp.concatenate(
+                [band_acc[head, 0, rows], band_acc[head, 1, rows], gap, band_acc[head, 2, rows]], 1
+            )
+            lines = lines + (pltpu.roll(piece, span - 8 * g, 1) if g else piece)
+        for bit in (1, 2, 4):
+            lines = jnp.where((row & bit) != 0, pltpu.roll(lines, span - bit, 1), lines)
+        gband_ref[0, head : head + 1, :] = jnp.sum(lines, 0, keepdims=True)
+        gfar_ref[0, head : head + 1, :] = jnp.sum(far_acc[head], 0, keepdims=True)
+
+
+def attend_back(info, far, projected, others, band, out, gout, lse):
+    rows = projected.shape[0]
+    pairs = HEADS // 2
+    width = 2 * HEAD_DIM
+    inner = HEADS * HEAD_DIM
+    col = lambda shift: pl.BlockSpec((rows, width), lambda p: (0, p + shift))
+    two = pl.BlockSpec((2, rows, width), lambda p: (0, 0, p))
+    return pl.pallas_call(
+        attend_back_kernel,
+        grid=(pairs,),
+        in_specs=[
+            pl.BlockSpec(memory_space=pltpu.SMEM),
+            pl.BlockSpec(memory_space=pltpu.SMEM),
+            col(0),
+            col(pairs),
+            col(2 * pairs),
+            col(0),
+            col(pairs),
+            pl.BlockSpec((2, 3, BLOCK, BLOCK), lambda p: (p, 0, 0, 0)),
+            col(0),
+            col(0),
+            pl.BlockSpec((1, 2, 2, BLOCK), lambda p: (p, 0, 0, 0)),
+        ],
+        out_specs=[
+            col(0),
+            two,
+            two,
+            pl.BlockSpec((1, 2, 4 * BLOCK), lambda p: (p, 0, 0)),
+            pl.BlockSpec((1, 2, BLOCK), lambda p: (p, 0, 0)),
+        ],
+        out_shape=[
+            jax.ShapeDtypeStruct((rows, inner), LOW),
+            jax.ShapeDtypeStruct((2, rows, inner), WIDE),
+            jax.ShapeDtypeStruct((2, rows, inner), LOW),
+            jax.ShapeDtypeStruct((pairs, 2, 4 * BLOCK), WIDE),
+            jax.ShapeDtypeStruct((pairs, 2, BLOCK), WIDE),
+        ],
+        scratch_shapes=[
+            pltpu.VMEM((4 * BLOCK, width), WIDE),
+            pltpu.VMEM((4 * BLOCK, width), WIDE),
+            pltpu.VMEM((2, 3, BLOCK, BLOCK), WIDE),
+            pltpu.VMEM((2, 8, BLOCK), WIDE),
+        ],
+        name="attend_back",
+    )(info, far, projected, projected, projected, others, others, band, out, gout, lse)
+
+
+def chip_body(
+    byte_states,
+    teacher,
+    lengths,
+    conv_taps,
+    conv_bias,
+    join_weight,
+    join_bias,
+    gain_attn,
+    attn_in_weight,
+    attn_out_weight,
+    position_bias,
+    gain_mlp,
+    mlp_in_weight,
+    mlp_out_weight,
+):
+    layer_count = conv_taps.shape[0]
+    model_width = byte_states.shape[3]
+    slot_rows = byte_states.shape[2]
+    rows = 2 * slot_rows
+    hidden_width = mlp_in_weight.shape[3]
+    quarters = hidden_width // model_width
+    seqs, zs, cores = (lax.axis_size(name) for name in ALL)
+    devices = seqs * zs * cores
+    share = model_width // devices
+    s_at, z_at, c_at = (lax.axis_index(name) for name in ALL)
+    device_at = (s_at * zs + z_at) * cores + c_at
+
+    def number(s, z, c):
+        return (s * zs + z) * cores + c
+
+    places = [(s, z, c) for s in range(seqs) for z in range(zs) for c in range(cores)]
+    swap = [(number(s, z, c), number(s, z, 1 - c)) for s, z, c in places]
+    routes = [
+        [(number(s, z, c), number(2 * (s % 2 if turn == 0 else 1 - s % 2) + c, z, s // 2)) for s, z, c in places]
+        for turn in range(2)
+    ]
+    back_routes = [[(b, a) for a, b in route] for route in routes]
+
+    def to_chips(block):
+        odd, high = s_at % 2, s_at // 2
+        first, second = (
+            lax.ppermute(jnp.where(odd == turn, block[0], block[1]), ALL, routes[turn]) for turn in range(2)
+        )
+        return jnp.concatenate(
+            [jnp.where(high == 0, first, second), jnp.where(high == 0, second, first)], 0
+        )
+
+    def from_chips(block):
+        odd, high = s_at % 2, s_at // 2
+        halves = (block[:slot_rows], block[slot_rows:])
+        first, second = (
+            lax.ppermute(jnp.where(high == turn, halves[0], halves[1]), ALL, back_routes[turn])
+            for turn in range(2)
+        )
+        return jnp.stack([jnp.where(odd == 0, first, second), jnp.where(odd == 0, second, first)])
+
+    def trade(block):
+        return lax.ppermute(block, ALL, swap)
+
+    to_high = [(number(s, z, 0), number(s, z, 1)) for s, z, c in places if c == 0]
+    to_low = [(b, a) for a, b in to_high]
+
+    lanes = jnp.arange(model_width)
+    lane_owner, lane_item = lanes // share, lanes % share
+    spread = (lanes[None, :] == device_at * share + jnp.arange(share)[:, None]).astype(LOW)
+    length_parts = jnp.stack([lengths[:, 0] // 32, lengths[:, 0] % 32], 1).reshape(-1)
+
+    def packed(l):
+        last = jnp.concatenate(
+            [
+                position_bias[l],
+                length_parts.astype(LOW),
+                jnp.zeros((share - HEADS - length_parts.shape[0],), LOW),
+            ]
+        )
+        small = jnp.concatenate(
+            [
+                conv_taps[l],
+                conv_bias[l],
+                join_bias[l][None],
+                gain_attn[l][None],
+                gain_mlp[l][None],
+                last[None],
+            ],
+            0,
+        )
+        small = jnp.dot(small, spread, preferred_element_type=WIDE).astype(LOW)
+        inward = mlp_in_weight[l].reshape(2, share, quarters, model_width)
+        return jnp.concatenate(
+            [
+                join_weight[l],
+                attn_in_weight[l].reshape(3 * share, model_width),
+                attn_out_weight[l],
+                inward.transpose(0, 2, 1, 3).reshape(2 * quarters * share, model_width),
+                mlp_out_weight[l],
+                small,
+            ],
+            0,
+        )
+
+    gathered = [
+        lax.all_gather(packed(l), ALL, axis=0, tiled=False).reshape(devices, -1, share, model_width)
+        for l in range(layer_count)
+    ]
+
+    def unpack(whole):
+        small = jnp.sum(whole[:, -1].astype(WIDE), 0)
+        square = lambda at: whole[:, at].reshape(model_width, model_width)
+        wide = lambda at, count: (
+            whole[:, at : at + count].transpose(0, 2, 1, 3).reshape(model_width, count * model_width)
+        )
+        return dict(
+            join=square(0),
+            attn_in=wide(1, 3),
+            attn_out=square(4),
+            gate=wide(5, quarters),
+            up=wide(5 + quarters, quarters),
+            mlp_out=whole[:, 5 + 2 * quarters : 5 + 3 * quarters].reshape(hidden_width, model_width),
+            taps=jnp.stack(
+                [
+                    small[5],
+                    small[2] + small[6],
+                    small[0] + small[3] + small[7],
+                    small[1] + small[4] + small[8],
+                ]
+            ),
+            bias=small[9] + small[10] + small[11],
+            join_bias=small[12],
+            gain_attn=small[13],
+            gain_mlp=small[14],
+            last=small[15],
+        )
+
+    weights = [unpack(whole) for whole in gathered]
+    state = to_chips(byte_states[:, 0]).astype(WIDE)
+    target = to_chips(teacher[:, 0])
+
+    counts = weights[0]["last"]
+    scale = jnp.where((lane_item >= HEADS) & (lane_item < HEADS + 4), jnp.where(lane_item % 2 == 0, 32.0, 1.0), 0.0)
+    total_valid = jnp.sum(jnp.where(lane_owner < zs * cores, counts * scale, 0.0))
+    mine = (lane_owner == z_at * cores + s_at % 2) & ((lane_item - HEADS) // 2 == s_at // 2)
+    length = jnp.sum(jnp.where(mine, counts * scale, 0.0)).astype(jnp.int32)
+    info = jnp.stack([c_at.astype(jnp.int32), length])
+    row_valid = (rows * c_at + jnp.arange(rows) < length)[:, None]
+
+    offsets = -((jnp.arange(4 * BLOCK) + 2 * BLOCK) % (4 * BLOCK) - 2 * BLOCK)
+    in_bucket = (lane_owner[:, None] == bucket_ids(offsets)[None, :]).astype(LOW)
+    of_head = (lane_item[None, :] == jnp.arange(HEADS)[:, None]).astype(WIDE)
+    far_bucket = (lane_owner == jnp.where(c_at == 0, 31, 15)).astype(WIDE)
+
+    def normed(values, gain):
+        inverse = lax.rsqrt(jnp.mean(values * values, -1, keepdims=True) + eps)
+        return (values * inverse * gain).astype(LOW)
+
+    def normed_back(grad, values, gain):
+        inverse = lax.rsqrt(jnp.mean(values * values, -1, keepdims=True) + eps)
+        unit = values * inverse
+        scaled = grad * gain
+        grad_in = inverse * (scaled - unit * jnp.mean(scaled * unit, -1, keepdims=True))
+        return grad_in, jnp.sum(grad * unit, 0)
+
+    kept = []
+    for l in range(layer_count):
+        w = weights[l]
+        low_state = state.astype(LOW)
+        prior = lax.ppermute(low_state[rows - 8 :], ALL, to_high)[5:]
+        extended = jnp.concatenate([prior, low_state], 0).astype(WIDE)
+        mixed = w["bias"] + sum(w["taps"][k] * extended[k : k + rows] for k in range(4))
+        mixed = mixed.astype(LOW)
+        joined = state + nn(mixed, w["join"]) + w["join_bias"]
+        norm_a = normed(joined, w["gain_attn"])
+        projected = nn(norm_a, w["attn_in"]).astype(LOW)
+        others = trade(projected[:, HEADS * HEAD_DIM :])
+        line = jnp.dot(
+            (of_head * w["last"]).astype(LOW), in_bucket, preferred_element_type=WIDE
+        )
+        far = jnp.sum(of_head * (w["last"] * far_bucket), 1)
+        band = build_band(line)
+        attended, lse = attend(info, far, projected, others, band)
+        mid = joined + nn(attended, w["attn_out"])
+        norm_m = normed(mid, w["gain_mlp"])
+        gate = nn(norm_m, w["gate"])
+        up = nn(norm_m, w["up"])
+        hidden = (jax.nn.gelu(gate, approximate=True) * up).astype(LOW)
+        state = mid + nn(hidden, w["mlp_out"])
+        kept.append(
+            (extended, mixed, joined, norm_a, projected, others, far, band, attended, lse, mid, norm_m, gate, up, hidden)
+        )
+
+    activations = from_chips(state)[:, None]
+    diff = jnp.where(row_valid, state - target.astype(WIDE), 0.0)
+    squares = jnp.sum(diff * diff, 0)
+    grad = 2.0 * diff / (total_valid * model_width)
+    results = [None] * layer_count
+    for l in reversed(range(layer_count)):
+        w = weights[l]
+        (extended, mixed, joined, norm_a, projected, others, far, band, attended, lse, mid, norm_m, gate, up, hidden) = kept[l]
+        g_low = grad.astype(LOW)
+        g_mlp_out = tn(hidden, g_low).astype(LOW)
+        g_hidden = nt(g_low, w["mlp_out"])
+        unused, gelu_back = jax.vjp(gated_unit, gate, up)
+        g_gate, g_up = (part.astype(LOW) for part in gelu_back(g_hidden))
+        g_in = [tn(norm_m, part).astype(LOW) for part in (g_gate, g_up)]
+        g_norm = nt(g_gate, w["gate"]) + nt(g_up, w["up"])
+        g_mid, g_gain_mlp = normed_back(g_norm, mid, w["gain_mlp"])
+        g_mid = grad + g_mid
+        g_mid_low = g_mid.astype(LOW)
+        g_attn_out = tn(attended, g_mid_low).astype(LOW)
+        g_att = nt(g_mid_low, w["attn_out"]).astype(LOW)
+        g_query, g_own, g_other, g_band, g_far = attend_back(
+            info, far, projected, others, band, attended, g_att, lse
+        )
+        g_kv = (g_own + trade(g_other).astype(WIDE)).astype(LOW)
+        g_proj = jnp.concatenate([g_query, g_kv[0], g_kv[1]], 1)
+        g_attn_in = tn(norm_a, g_proj).astype(LOW)
+        g_norm = nt(g_proj, w["attn_in"])
+        g_joined, g_gain_attn = normed_back(g_norm, joined, w["gain_attn"])
+        g_joined = g_mid + g_joined
+        g_join_low = g_joined.astype(LOW)
+        g_join = tn(mixed, g_join_low).astype(LOW)
+        g_join_bias = jnp.sum(g_join_low.astype(WIDE), 0)
+        g_mixed = nt(g_join_low, w["join"]).astype(LOW).astype(WIDE)
+        g_taps = [jnp.sum(g_mixed * extended[k : k + rows], 0) for k in range(4)]
+        g_bias = jnp.sum(g_mixed, 0)
+        head_rows = [
+            sum(w["taps"][k] * g_mixed[r - k : r - k + 1] for k in range(r + 1)) for r in range(3)
+        ]
+        beyond = lax.ppermute(
+            jnp.concatenate(head_rows + [jnp.zeros((5, model_width), WIDE)], 0), ALL, to_low
+        )
+        padded = jnp.concatenate([g_mixed, jnp.zeros((3, model_width), WIDE)], 0)
+        g_state = sum(w["taps"][k] * padded[3 - k : 3 - k + rows] for k in range(4))
+        tail = jnp.concatenate([jnp.zeros((rows - 8, model_width), WIDE), jnp.zeros((5, model_width), WIDE), beyond[:3]], 0)
+        grad = g_joined + g_state + tail
+
+        by_lane = jnp.dot(
+            g_band.reshape(HEADS, -1),
+            in_bucket.T.astype(WIDE),
+            precision=lax.Precision.HIGHEST,
+            preferred_element_type=WIDE,
+        )
+        g_far = jnp.sum(g_far.reshape(HEADS, -1), 1)[:, None]
+        g_last = jnp.sum(of_head * (by_lane + g_far * far_bucket), 0)
+        small = jnp.stack(
+            g_taps
+            + [g_bias, g_join_bias, g_gain_attn, g_gain_mlp, g_last, squares]
+            + [jnp.zeros((model_width,), WIDE)] * (share - 10)
+        ).astype(LOW)
+        split = lambda whole: whole.reshape(devices, share, -1, model_width).transpose(0, 2, 1, 3)
+        terms = jnp.concatenate(
+            [
+                split(g_join),
+                split(g_attn_in),
+                split(g_attn_out),
+                split(g_in[0]),
+                split(g_in[1]),
+                g_mlp_out.reshape(devices, quarters, share, model_width),
+                jnp.broadcast_to(small[None, None], (devices, 1, share, model_width)),
+            ],
+            1,
+        ).reshape(seqs, zs, cores, -1, model_width)
+        kept_half = jnp.where(c_at == 0, terms[:, :, 0], terms[:, :, 1])
+        sent_half = jnp.where(c_at == 0, terms[:, :, 1], terms[:, :, 0])
+        half = (kept_half.astype(WIDE) + trade(sent_half).astype(WIDE)).astype(LOW)
+        half = lax.psum_scatter(half, "seq", scatter_dimension=0, tiled=False)
+        results[l] = lax.psum_scatter(half, "z", scatter_dimension=0, tiled=False)
+
+    input_grad = from_chips(grad)[:, None]
+    owned = [result.astype(WIDE).reshape(-1, share, model_width) for result in results]
+    small = [lax.dynamic_slice_in_dim(part[-1], device_at * share, share, 1) for part in owned]
+    stack = lambda pick: jnp.stack([pick(l) for l in range(layer_count)])
+    taps_at = (2, 3, 1, 2, 3, 0, 1, 2, 3)
+    loss = jnp.sum(owned[-1][-1][9]) / (total_valid * model_width)
+    inward = lambda part: part.transpose(1, 0, 2).reshape(share, hidden_width)
+    return (
+        activations,
+        loss,
+        input_grad,
+        stack(lambda l: jnp.stack([small[l][k] for k in taps_at])),
+        stack(lambda l: jnp.broadcast_to(small[l][4], (3, share))),
+        stack(lambda l: owned[l][0]),
+        stack(lambda l: small[l][5]),
+        stack(lambda l: small[l][6]),
+        stack(lambda l: owned[l][1:4]),
+        stack(lambda l: owned[l][4]),
+        stack(lambda l: small[l][8][:HEADS]),
+        stack(lambda l: small[l][7]),
+        stack(
+            lambda l: jnp.stack(
+                [inward(owned[l][5 : 5 + quarters]), inward(owned[l][5 + quarters : 5 + 2 * quarters])]
+            )
+        ),
+        stack(lambda l: owned[l][5 + 2 * quarters : 5 + 3 * quarters].reshape(-1, model_width)),
+    )
+
+
+def chip_plan(mesh):
+    grid = Mesh(
+        mesh.devices.reshape(mesh.shape["seq"], mesh.shape["batch"] // 2, 2),
+        ALL,
+    )
+    batch = ("z", "core")
+    in_specs = (
+        P(None, batch, "seq", None),
+        P(None, batch, "seq", None),
+        P(None, batch),
+        P(None, None, ALL),
+        P(None, None, ALL),
+        P(None, ALL, None),
+        P(None, ALL),
+        P(None, ALL),
+        P(None, None, ALL, None),
+        P(None, ALL, None),
+        P(None, ALL),
+        P(None, ALL),
+        P(None, None, ALL, None),
+        P(None, ALL, None),
+    )
+    out_specs = (in_specs[0], P(), in_specs[0]) + in_specs[3:]
+    return jax.shard_map(chip_body, mesh=grid, in_specs=in_specs, out_specs=out_specs, check_vma=False)
+
+
+def shared_plan(mesh):
     in_specs = (
         P(None, "batch", "seq", None),
         P(None, "batch", "seq", None),
@@ -445,3 +1047,16 @@
         P(None, ("seq", "batch"), None),
     )
     return jax.shard_map(body, mesh=mesh, in_specs=in_specs, out_specs=out_specs, check_vma=False)
+
+
+def solution(mesh):
+    shared = shared_plan(mesh)
+
+    def run(*arrays):
+        sequences = arrays[0].shape[0] * arrays[0].shape[1]
+        one_per_chip = 2 * sequences == mesh.devices.size and 2 * arrays[0].shape[0] == mesh.shape["seq"]
+        lanes_fit = arrays[5].shape[1] == 16 * mesh.devices.size and arrays[0].shape[2] == 4 * BLOCK
+        plan = chip_plan(mesh) if one_per_chip and lanes_fit else shared
+        return plan(*arrays)
+
+    return run

time: 2580 us -> 657 us (0.25)
  waiting for transfers between devices: 1500 us -> 264 us
  blocking collectives: 414 us -> 0 us
  matrix products: 280 us -> 80 us
  local copies, waits for them, and re-layouts: 258 us -> 118 us
  Pallas kernels: 0 us -> 75.7 us
    unnamed x37 -> x8, waiting for transfers between devices: 872 us -> 77.5 us
    reduce_scatter x11 -> x2, waiting for transfers between devices: 516 us -> 53.7 us  [chip_body(): results[l] = lax.psum_scatter(half, 'z', scatter_dimension=0, tiled=False)]
    all_gather x8 -> x0, blocking collectives: 319 us -> none  [the longest x2 84.6 us: body(): lax.all_gather(attn_out_weight[layer_index], ('seq', 'batch'), axis=0, ti...]
    dot_general x90 -> x42, matrix products: 280 us -> 80 us  [the longest x12 34.5 us: tn(): lax.dot_general(left, right, (((0,), (0,)), ((), ())), preferred_element_...]
    pallas_call x0 -> x6, Pallas kernels: none -> 75.7 us  [the longest x2 39.7 us: attend_back(): pl.pallas_call(attend_back_kernel, grid=(pairs,), in_specs=[pl.BlockSpec(...]
    psum x2 -> x0, blocking collectives: 54.1 us -> none  [the longest x1 39.3 us: body(): lax.psum(local_squares, ('seq', 'batch')) / (total_valid * model_width)]
    convert_element_type x16 -> x1, local copies, waits for them, and re-layouts: 49.5 us -> 0.09 us  [packed(): length_parts.astype(LOW)]
    eq x1 -> x0, local copies, waits for them, and re-layouts: 46.1 us -> none  [body(): bucket_grid[:, :, None] == jnp.arange(BUCKETS)[None, None, :]]
  transfers between devices with their start and end apart: 39 -> 24, of which waited for: 19 -> 9; matrix products, arithmetic and copies ran while one was open for 20% -> 28% of each run, Pallas kernels for 0% -> 7%
where the time goes in v1:
time: 657 us; the launch traced here: 648 us
  waiting for transfers between devices  264 us (40%)
  local copies, waits for them, and re-layouts  118 us (18%)
  matrix products  80 us (12%)
  Pallas kernels  75.7 us (12%)
  other arithmetic  63.4 us (10%)
  starting transfers between devices  28 us (4%)
  between operations  19.1 us (3%)
    all_gather x2, waiting for transfers between devices, chip_body(): lax.all_gather(packed(l), ALL, axis=0, tiled=False)  120 us
    unnamed x8, waiting for transfers between devices  77.5 us
    reduce_scatter x2, waiting for transfers between devices, chip_body(): results[l] = lax.psum_scatter(half, 'z', scatter_dimension=0, tiled=False)  53.7 us
    unnamed x222, local copies, waits for them, and re-layouts  49.7 us
    pallas_call x2, Pallas kernels, attend_back(): pl.pallas_call(attend_back_kernel, grid=(pairs,), in_specs=[pl.BlockSpec(...  39.7 us
    dot_general x12, matrix products, tn(): lax.dot_general(left, right, (((0,), (0,)), ((), ())), preferred_element_...  34.5 us
    reshape x6, local copies, waits for them, and re-layouts, chip_body(): whole.reshape(devices, share, -1, model_width).transpose(0, 2, 1, 3)  29.9 us
    pallas_call x2, Pallas kernels, attend(): pl.pallas_call(attend_kernel, grid=(pairs,), in_specs=[pl.BlockSpec(memor...  23.9 us
  transfers between devices with their start and end apart: 24, of which 9 were waited for; matrix products, arithmetic and copies ran while one was open for 28% of the time, Pallas kernels for 7%

profile of v1, /device:TPU:0, one launch (start us, length us, event | category | flops | bytes accessed | tf_op | source)
XLA Modules:
  0.0 648.4 jit_solution(1515184827137608803)
XLA Ops:
  17.9 4.3 collective-permute-start.1
  22.9 3.6 collective-permute-start.8
  27.6 4.3 collective-permute-done.1
  34.2 69.3 %all-gather.5.cloned.1.call-done = bf16[9216,512]{1,0:T(8,128)(2,1)} async-done(((bf16[288,512]{1,0:T(8,128)(2,1)}), bf16[9216,512]{1,0:T(8,128)(2,1)}) %all-gather.5.cloned.1.call-update) | async-done | bytes 9437200 | tf_op jit(solution)/shard_map/all_gather | solution.py:795
  108.7 2.1 fusion.144
  117.1 6.4 bias_band.2.band_ref
  123.5 5.5 fusion.143
  136.2 50.4 %all-gather.7.cloned.1.call-done = bf16[9216,512]{1,0:T(8,128)(2,1)} async-done(((bf16[288,512]{1,0:T(8,128)(2,1)}), bf16[9216,512]{1,0:T(8,128)(2,1)}) %all-gather.7.cloned.1.call-update) | async-done | bytes 9437200 | tf_op jit(solution)/shard_map/all_gather | solution.py:795
  189.5 11.9 %attend.2 = (bf16[512,512]{1,0:T(8,128)(2,1)}, f32[4,2,2,256]{3,2,1,0:T(2,128)}) custom-call(s32[2]{0:T(128)} %pad_add_fusion.info_ref, f32[8]{0:T(128)} %get-tuple-element.117.far_ref, bf16[512,1536]{1,0:T(8,128)(2,1)} %copy-done.2, bf16[512,1536]{1,0:T(8,128)(2,1)} %copy-done.2, bf16[512,1536]{1,0:T(8,128)(2,1)} %copy-done.2, bf16[512,1024]{1,0:T(8,128)(2,1)} %copy-done.6, ...), custom_call_target="tpu_custom_call" | custom-call | tf_op jit(solution)/shard_map/attend/pallas_call | solution.py:522
  205.6 3.4 multiply_convert_fusion.3
  210.3 2.3 collective-permute-start.4
  224.5 5.8 bias_band.3.band_ref
  230.3 5.5 fusion.141
  244.4 12.0 %attend.3 = (bf16[512,512]{1,0:T(8,128)(2,1)}, f32[4,2,2,256]{3,2,1,0:T(2,128)}) custom-call(s32[2]{0:T(128)} %pad_add_fusion.info_ref, f32[8]{0:T(128)} %get-tuple-element.116.far_ref, bf16[512,1536]{1,0:T(8,128)(2,1)} %copy-done.3, bf16[512,1536]{1,0:T(8,128)(2,1)} %copy-done.3, bf16[512,1536]{1,0:T(8,128)(2,1)} %copy-done.3, ...), custom_call_target="tpu_custom_call" | custom-call | tf_op jit(solution)/shard_map/attend/pallas_call | solution.py:522
  260.1 2.1 multiply_convert_fusion.2
  263.5 5.5 multiply_convert_fusion.1
  270.3 2.6 convolution_convert_fusion.8
  277.3 19.8 %attend_back.2 = (bf16[512,512]{1,0:T(8,128)(2,1)}, f32[2,512,512]{2,1,0:T(8,128)}, bf16[2,512,512]{2,1,0:T(8,128)(2,1)}, f32[4,2,1024]{2,1,0:T(2,128)}, f32[4,2,256]{2,1,0:T(2,128)}) custom-call(s32[2]{0:T(128)} %pad_add_fusion.info_ref, f32[8]{0:T(128)} %get-tuple-element.116.far_ref, bf16[512,1536]{1,0:T(8,128)(2,1)} %copy-done.3, ...), custom_call_target="tpu_custom_call" | custom-call | tf_op jit(solution)/shard_map/attend_back/pallas_call | solution.py:653
  302.2 4.5 reshape.604
  306.7 4.4 convolution_convert_fusion.9
  311.1 4.6 reshape.603
  315.7 2.3 convolution_convert_fusion.15
  318.0 4.8 convolution_convert_fusion.7
  325.8 2.3 convolution_convert_fusion.1
  333.0 5.6 reshape.602
  340.6 3.4 copy_dynamic-update-slice_fusion.1
  345.0 2.1 bitcast_dynamic-update-slice_fusion.3
  350.7 2.1 fusion.50
  353.8 6.8 %fusion.2 = bf16[4,4,288,512]{3,2,1,0:T(8,128)(2,1)} fusion(pred[]{:T(512)S(6)} %eq.182, bf16[4,4,2,288,512]{4,3,2,1,0:T(8,128)(2,1)} %bitcast.72), kind=kLoop, calls=%fused_computation.9 | loop fusion | flops 2359296 | bytes 14155777 | tf_op jit(solution)/shard_map/jit(_where)/select_n | solution.py:956
  362.7 4.0 multiply_convert_fusion
  374.0 19.9 %attend_back.3 = (bf16[512,512]{1,0:T(8,128)(2,1)}, f32[2,512,512]{2,1,0:T(8,128)}, bf16[2,512,512]{2,1,0:T(8,128)(2,1)}, f32[4,2,1024]{2,1,0:T(2,128)}, f32[4,2,256]{2,1,0:T(2,128)}) custom-call(s32[2]{0:T(128)} %pad_add_fusion.info_ref, f32[8]{0:T(128)} %get-tuple-element.117.far_ref, bf16[512,1536]{1,0:T(8,128)(2,1)} %copy-done.2, ...), custom_call_target="tpu_custom_call" | custom-call | tf_op jit(solution)/shard_map/attend_back/pallas_call | solution.py:653
  396.7 4.2 convolution_convert_fusion.6
  402.0 4.5 reshape.609
  406.5 4.3 convolution_convert_fusion.5
  410.8 5.0 reshape.610
  417.0 4.4 convolution_convert_fusion.4
  425.7 9.5 %fusion.1 = bf16[4,4,288,512]{3,2,1,0:T(8,128)(2,1)} fusion(bf16[4,4,288,512]{3,2,1,0:T(8,128)(2,1)} %collective-permute-done.11, pred[]{:T(512)S(6)} %eq.182, bf16[4,4,2,288,512]{4,3,2,1,0:T(8,128)(2,1)} %bitcast.72), kind=kLoop, calls=%fused_computation.3 | loop fusion | flops 11796480 | bytes 18874368 | tf_op jit(solution)/shard_map/convert_element_type | solution.py:957
  440.3 2.3 convolution_convert_fusion
  442.5 5.8 reshape.608
  455.6 2.5 fusion.60
  460.3 4.5 select_bitcast_fusion
  465.8 7.7 %collective-permute-done.17 = bf16[4,4,288,512]{3,2,1,0:T(8,128)(2,1)} collective-permute-done((bf16[4,4,288,512]{3,2,1,0:T(8,128)(2,1)S(1)}, bf16[4,4,288,512]{3,2,1,0:T(8,128)(2,1)}, u32[]{:S(2)}, u32[]{:S(2)}) %collective-permute-start.17) | collective-permute-done | bytes 4718624 | tf_op jit(solution)/shard_map/ppermute | solution.py:751
  473.5 7.5 %fusion = bf16[4,4,288,512]{3,2,1,0:T(8,128)(2,1)} fusion(bf16[4,4,288,512]{3,2,1,0:T(8,128)(2,1)} %collective-permute-done.17, pred[]{:T(512)S(6)} %eq.182, bf16[4,4,2,288,512]{4,3,2,1,0:T(8,128)(2,1)S(1)} %bitcast.302), kind=kLoop, calls=%fused_computation.1 | loop fusion | flops 11796480 | bytes 18874368 | tf_op jit(solution)/shard_map/convert_element_type | solution.py:957
  481.1 9.7 %reduce-scatter.13.cloned.1.call-done = bf16[1,4,288,512]{3,2,1,0:T(8,128)(2,1)} async-done(((bf16[4,4,288,512]{3,2,1,0:T(8,128)(2,1)}), bf16[1,4,288,512]{3,2,1,0:T(8,128)(2,1)}) %reduce-scatter.13.cloned.1.call-update) | async-done | bytes 1179664
  497.8 2.7 collective-permute-start.16
  500.5 67.7 %reduce-scatter.15.cloned.1.call-done = bf16[1,4,288,512]{3,2,1,0:T(8,128)(2,1)} async-done(((bf16[4,4,288,512]{3,2,1,0:T(8,128)(2,1)}), bf16[1,4,288,512]{3,2,1,0:T(8,128)(2,1)}) %reduce-scatter.15.cloned.1.call-update) | async-done | bytes 1179664
  570.6 29.2 %reduce-scatter.9.cloned.1.call-done = bf16[1,288,512]{2,1,0:T(8,128)(2,1)} async-done(((bf16[4,288,512]{2,1,0:T(8,128)(2,1)}), bf16[1,288,512]{2,1,0:T(8,128)(2,1)}) %reduce-scatter.9.cloned.1.call-update) | async-done | bytes 294928 | tf_op jit(solution)/shard_map/reduce_scatter | solution.py:959
  605.4 24.5 %reduce-scatter.11.cloned.1.call-done = bf16[1,288,512]{2,1,0:T(8,128)(2,1)} async-done(((bf16[4,288,512]{2,1,0:T(8,128)(2,1)}), bf16[1,288,512]{2,1,0:T(8,128)(2,1)}) %reduce-scatter.11.cloned.1.call-update) | async-done | bytes 294928 | tf_op jit(solution)/shard_map/reduce_scatter | solution.py:959
  (451 shorter events, 149.8 us)
Async XLA Ops:
  7.2 7.7 %copy-start.83 = (bf16[2,16]{1,0:T(2,128)(2,1)S(1)}, bf16[2,16]{1,0:T(2,128)(2,1)}, u32[]{:S(2)}) copy-start(bf16[2,16]{1,0:T(2,128)(2,1)} %param.21) | copy-start | bytes 196
  7.2 7.7 %copy-start.82 = (bf16[2,16]{1,0:T(2,128)(2,1)S(1)}, bf16[2,16]{1,0:T(2,128)(2,1)}, u32[]{:S(2)}) copy-start(bf16[2,16]{1,0:T(2,128)(2,1)} %param.25) | copy-start | bytes 196
  7.2 7.7 %copy-start.71 = (bf16[2,64,512]{2,1,0:T(8,128)(2,1)S(1)}, bf16[2,64,512]{2,1,0:T(8,128)(2,1)}, u32[]{:S(2)}) copy-start(bf16[2,64,512]{2,1,0:T(8,128)(2,1)} %param.27) | copy-start | bytes 393220
  7.2 9.9 %copy-start.62 = (bf16[2,1,256,512]{3,2,1,0:T(8,128)(2,1)S(1)}, bf16[2,1,256,512]{3,2,1,0:T(8,128)(2,1)}, u32[]{:S(2)}) copy-start(bf16[2,1,256,512]{3,2,1,0:T(8,128)(2,1)} %param.14) | copy-start | bytes 1572868
  7.2 96.3 %all-gather.5.cloned.1.call-start = ((), (), s32[]{:S(2)}) async-start(), calls=%async_computation.6 | async-start | bytes 9732096 | tf_op jit(solution)/shard_map/all_gather | solution.py:795
  8.1 14.1 %copy-start.63 = (bf16[2,1,256,512]{3,2,1,0:T(8,128)(2,1)S(1)}, bf16[2,1,256,512]{3,2,1,0:T(8,128)(2,1)}, u32[]{:S(2)}) copy-start(bf16[2,1,256,512]{3,2,1,0:T(8,128)(2,1)} %param.15) | copy-start | bytes 1572868
  16.0 170.6 %all-gather.7.cloned.1.call-start = ((), (), s32[]{:S(2)}) async-start(), calls=%async_computation.7 | async-start | bytes 9732096 | tf_op jit(solution)/shard_map/all_gather | solution.py:795
  17.1 473.7 %reduce-scatter.13.cloned.1.call-start = ((), (), s32[]{:S(2)}) async-start(), calls=%async_computation.8 | async-start | bytes 5898240
  17.2 10.4 %collective-permute-start = (bf16[256,512]{1,0:T(8,128)(2,1)S(1)}, bf16[256,512]{1,0:T(8,128)(2,1)S(1)}, u32[]{:S(2)}, u32[]{:S(2)}) collective-permute-start(bf16[256,512]{1,0:T(8,128)(2,1)S(1)} %get-tuple-element.170), channel_id=1, source_target_pairs={{0,0},{1,8},{2,2},{3,10},{4,4},{5,12},{6,6},{7,14},{8,16},{9,24},{... | collective-permute-start | bytes 786440 | tf_op jit(solution)/shard_map/ppermute | solution.py:735
  17.9 14.0 %collective-permute-start.1 = (bf16[256,512]{1,0:T(8,128)(2,1)S(1)}, bf16[256,512]{1,0:T(8,128)(2,1)S(1)}, u32[]{:S(2)}, u32[]{:S(2)}) collective-permute-start(bf16[256,512]{1,0:T(8,128)(2,1)S(1)} %get-tuple-element.171), channel_id=1, source_target_pairs={{0,16},{1,24},{2,18},{3,26},{4,20},{5,28},{6,22},{7,30},{8,0},{9,8... | collective-permute-start | bytes 786440 | tf_op jit(solution)/shard_map/ppermute | solution.py:735
  22.9 198.7 %collective-permute-start.8 = (bf16[256,512]{1,0:T(8,128)(2,1)}, bf16[256,512]{1,0:T(8,128)(2,1)}, u32[]{:S(2)}, u32[]{:S(2)}) collective-permute-start(bf16[256,512]{1,0:T(8,128)(2,1)} %get-tuple-element.166), channel_id=1, source_target_pairs={{0,0},{1,8},{2,2},{3,10},{4,4},{5,12},{6,6},{7,14},{8,16},{9,24},{... | collective-permute-start | bytes 786440 | tf_op jit(solution)/shard_map/ppermute | solution.py:735
  26.5 195.1 %collective-permute-start.9 = (bf16[256,512]{1,0:T(8,128)(2,1)S(1)}, bf16[256,512]{1,0:T(8,128)(2,1)}, u32[]{:S(2)}, u32[]{:S(2)}) collective-permute-start(bf16[256,512]{1,0:T(8,128)(2,1)S(1)} %get-tuple-element.167), channel_id=1, source_target_pairs={{0,16},{1,24},{2,18},{3,26},{4,20},{5,28},{6,22},{7,30},{8,0},{9,8... | collective-permute-start | bytes 786440 | tf_op jit(solution)/shard_map/ppermute | solution.py:735
  27.6 195.8 %copy-start.80 = (s32[512]{0:T(512)}, s32[512]{0:T(512)S(1)}, u32[]{:S(2)}) copy-start(s32[512]{0:T(512)S(1)} %get-tuple-element.263) | copy-start | bytes 6148
  31.9 2.1 collective-permute-start.2
  34.2 76.5 %copy-start = (f32[515,512]{1,0:T(8,128)}, f32[515,512]{1,0:T(8,128)S(1)}, u32[]{:S(2)}) copy-start(f32[515,512]{1,0:T(8,128)S(1)} %maximum_convert_fusion) | copy-start | bytes 3164164
  113.2 10.3 %copy-start.2 = (bf16[512,1536]{1,0:T(8,128)(2,1)}, bf16[512,1536]{1,0:T(8,128)(2,1)S(1)}, u32[]{:S(2)}) copy-start(bf16[512,1536]{1,0:T(8,128)(2,1)S(1)} %convolution_convert_fusion.3.q_ref.k_ref.v_ref) | copy-start | bytes 4718596
  114.5 74.0 %collective-permute-start.3 = (bf16[512,1024]{1,0:T(8,128)(2,1)}, bf16[512,1024]{1,0:T(8,128)(2,1)S(1)}, u32[]{:S(2)}, u32[]{:S(2)}) collective-permute-start(bf16[512,1024]{1,0:T(8,128)(2,1)} %slice.743), channel_id=1, source_target_pairs={{0,1},{1,0},{2,3},{3,2},{4,5},{5,4},{6,7},{7,6},{8,9},{9,8},{10,11... | collective-permute-start | bytes 3145736 | tf_op jit(solution)/shard_map/ppermute | solution.py:751
  131.6 72.0 %copy-start.13 = (bf16[64,8,4,512]{3,1,2,0:T(8,128)(2,1)}, bf16[64,8,4,512]{3,1,2,0:T(8,128)(2,1)S(1)}, u32[]{:S(2)}) copy-start(bf16[64,8,4,512]{3,1,2,0:T(8,128)(2,1)S(1)} %copy.156) | copy-start | bytes 6291460
  210.3 7.6 %collective-permute-start.4 = (bf16[8,512]{1,0:T(8,128)(2,1)S(1)}, bf16[8,512]{1,0:T(8,128)(2,1)S(1)}, u32[]{:S(2)}, u32[]{:S(2)}) collective-permute-start(bf16[8,512]{1,0:T(8,128)(2,1)S(1)} %slice.754), channel_id=1, source_target_pairs={{0,1},{2,3},{4,5},{6,7},{8,9},{10,11},{12,13},{14,15},{16,17},{18,... | collective-permute-start | bytes 24584 | tf_op jit(solution)/shard_map/ppermute | solution.py:859
  213.9 42.4 %copy-start.26 = (bf16[32,1,16,512]{3,2,1,0:T(8,128)(2,1)}, bf16[32,1,16,512]{3,2,1,0:T(8,128)(2,1)S(1)}, u32[]{:S(2)}) copy-start(bf16[32,1,16,512]{3,2,1,0:T(8,128)(2,1)S(1)} %get-tuple-element.127) | copy-start | bytes 1572868
  220.2 10.1 %copy-start.3 = (bf16[512,1536]{1,0:T(8,128)(2,1)}, bf16[512,1536]{1,0:T(8,128)(2,1)S(1)}, u32[]{:S(2)}) copy-start(bf16[512,1536]{1,0:T(8,128)(2,1)S(1)} %convolution_convert_fusion.2.q_ref.k_ref.v_ref) | copy-start | bytes 4718596
  221.6 22.8 %collective-permute-start.5 = (bf16[512,1024]{1,0:T(8,128)(2,1)}, bf16[512,1024]{1,0:T(8,128)(2,1)}, u32[]{:S(2)}, u32[]{:S(2)}) collective-permute-start(bf16[512,1024]{1,0:T(8,128)(2,1)} %slice.773), channel_id=1, source_target_pairs={{0,1},{1,0},{2,3},{3,2},{4,5},{5,4},{6,7},{7,6},{8,9},{9,8},{10,11... | collective-permute-start | bytes 3145736 | tf_op jit(solution)/shard_map/ppermute | solution.py:751
  244.3 30.6 %copy-start.84 = (pred[512]{0:T(512)(128)(4,1)}, pred[512]{0:T(512)(128)(4,1)S(1)}, u32[]{:S(2)}) copy-start(pred[512]{0:T(512)(128)(4,1)S(1)} %add_compare_fusion) | copy-start | bytes 1540
  244.4 12.0 %copy-start.10 = (f32[512,512]{1,0:T(8,128)S(1)}, f32[512,512]{1,0:T(8,128)}, u32[]{:S(2)}) copy-start(f32[512,512]{1,0:T(8,128)} %copy-done.9) | copy-start | bytes 3145732
  258.3 12.1 %copy-start.56 = (bf16[512,512]{1,0:T(8,128)(2,1)}, bf16[512,512]{1,0:T(8,128)(2,1)S(1)}, u32[]{:S(2)}) copy-start(bf16[512,512]{1,0:T(8,128)(2,1)S(1)} %multiply_convert_fusion.4) | copy-start | bytes 1572868
  263.5 11.5 %copy-start.34 = (f32[512,512]{1,0:T(8,128)}, f32[512,512]{1,0:T(8,128)S(1)}, u32[]{:S(2)}) copy-start(f32[512,512]{1,0:T(8,128)S(1)} %convolution_add_fusion.5) | copy-start | bytes 3145732
  297.0 25.8 %collective-permute-start.10 = (bf16[2,512,512]{2,1,0:T(8,128)(2,1)}, bf16[2,512,512]{2,1,0:T(8,128)(2,1)}, u32[]{:S(2)}, u32[]{:S(2)}) collective-permute-start(bf16[2,512,512]{2,1,0:T(8,128)(2,1)} %get-tuple-element.33), channel_id=1, source_target_pairs={{0,1},{1,0},{2,3},{3,2},{4,5},{5,4},{6,7},{7,6},{8,9},{9,8},{10,11... | collective-permute-start | bytes 3145736 | tf_op jit(solution)/shard_map/ppermute | solution.py:751
  311.1 7.0 %copy-start.85 = (pred[512]{0:T(512)(128)(4,1)S(1)}, pred[512]{0:T(512)(128)(4,1)}, u32[]{:S(2)}) copy-start(pred[512]{0:T(512)(128)(4,1)} %copy-done.84) | copy-start | bytes 1540
  331.7 18.9 %collective-permute-start.12 = (f32[8,512]{1,0:T(8,128)S(1)}, f32[8,512]{1,0:T(8,128)S(1)}, u32[]{:S(2)}, u32[]{:S(2)}) collective-permute-start(f32[8,512]{1,0:T(8,128)S(1)} %pad_maximum_fusion.14), channel_id=1, source_target_pairs={{1,0},{3,2},{5,4},{7,6},{9,8},{11,10},{13,12},{15,14},{17,16},{19,... | collective-permute-start | bytes 49160 | tf_op jit(solution)/shard_map/ppermute | solution.py:921
  353.8 7.9 %copy-start.28 = (f32[512,512]{1,0:T(8,128)S(1)}, f32[512,512]{1,0:T(8,128)}, u32[]{:S(2)}) copy-start(f32[512,512]{1,0:T(8,128)} %get-tuple-element.161) | copy-start | bytes 3145732
  353.8 7.9 %copy-start.33 = (f32[512,2048]{1,0:T(8,128)S(1)}, f32[512,2048]{1,0:T(8,128)}, u32[]{:S(2)}) copy-start(f32[512,2048]{1,0:T(8,128)} %copy-done.32) | copy-start | bytes 12582916
  353.8 7.9 %copy-start.50 = (bf16[32,4,16,512]{3,2,1,0:T(8,128)(2,1)S(1)}, bf16[32,4,16,512]{3,2,1,0:T(8,128)(2,1)}, u32[]{:S(2)}) copy-start(bf16[32,4,16,512]{3,2,1,0:T(8,128)(2,1)} %get-tuple-element.129) | copy-start | bytes 6291460
  353.8 8.8 %copy-start.94 = (f32[512,2048]{1,0:T(8,128)S(1)}, f32[512,2048]{1,0:T(8,128)}, u32[]{:S(2)}) copy-start(f32[512,2048]{1,0:T(8,128)} %get-tuple-element.241) | copy-start | bytes 12582916
  360.7 65.0 %collective-permute-start.11 = (bf16[4,4,288,512]{3,2,1,0:T(8,128)(2,1)}, bf16[4,4,288,512]{3,2,1,0:T(8,128)(2,1)}, u32[]{:S(2)}, u32[]{:S(2)}) collective-permute-start(bf16[4,4,288,512]{3,2,1,0:T(8,128)(2,1)} %fusion.2), channel_id=1, source_target_pairs={{0,1},{1,0},{2,3},{3,2},{4,5},{5,4},{6,7},{7,6},{8,9},{9,8},{10,11... | collective-permute-start | bytes 14155784 | tf_op jit(solution)/shard_map/ppermute | solution.py:751
  374.0 22.7 %copy-start.55 = (bf16[512,512]{1,0:T(8,128)(2,1)S(1)}, bf16[512,512]{1,0:T(8,128)(2,1)}, u32[]{:S(2)}) copy-start(bf16[512,512]{1,0:T(8,128)(2,1)} %copy-done.54) | copy-start | bytes 1572868
  395.6 25.9 %collective-permute-start.13 = (bf16[2,512,512]{2,1,0:T(8,128)(2,1)}, bf16[2,512,512]{2,1,0:T(8,128)(2,1)}, u32[]{:S(2)}, u32[]{:S(2)}) collective-permute-start(bf16[2,512,512]{2,1,0:T(8,128)(2,1)} %get-tuple-element.39), channel_id=1, source_target_pairs={{0,1},{1,0},{2,3},{3,2},{4,5},{5,4},{6,7},{7,6},{8,9},{9,8},{10,11... | collective-permute-start | bytes 3145736 | tf_op jit(solution)/shard_map/ppermute | solution.py:751
  435.2 133.1 %reduce-scatter.15.cloned.1.call-start = ((), (), s32[]{:S(2)}) async-start(), calls=%async_computation.9 | async-start | bytes 5898240
  439.0 16.4 %collective-permute-start.14 = (f32[8,512]{1,0:T(8,128)S(1)}, f32[8,512]{1,0:T(8,128)S(1)}, u32[]{:S(2)}, u32[]{:S(2)}) collective-permute-start(f32[8,512]{1,0:T(8,128)S(1)} %pad_maximum_fusion.13), channel_id=1, source_target_pairs={{1,0},{3,2},{5,4},{7,6},{9,8},{11,10},{13,12},{15,14},{17,16},{19,... | collective-permute-start | bytes 49160 | tf_op jit(solution)/shard_map/ppermute | solution.py:921
  460.3 13.2 %copy-start.5 = (bf16[32,18,16,512]{3,2,1,0:T(8,128)(2,1)S(1)}, bf16[32,18,16,512]{3,2,1,0:T(8,128)(2,1)}, u32[]{:S(2)}) copy-start(bf16[32,18,16,512]{3,2,1,0:T(8,128)(2,1)} %broadcast_dynamic-update-slice_fusion) | copy-start | bytes 28311556
  464.8 8.7 %collective-permute-start.17 = (bf16[4,4,288,512]{3,2,1,0:T(8,128)(2,1)S(1)}, bf16[4,4,288,512]{3,2,1,0:T(8,128)(2,1)}, u32[]{:S(2)}, u32[]{:S(2)}) collective-permute-start(bf16[4,4,288,512]{3,2,1,0:T(8,128)(2,1)S(1)} %select_bitcast_fusion), channel_id=1, source_target_pairs={{0,1},{1,0},{2,3},{3,2},{4,5},{5,4},{6,7},{7,6},{8,9},{9,8},{10,11... | collective-permute-start | bytes 14155784 | tf_op jit(solution)/shard_map/ppermute | solution.py:751
  481.1 9.8 %copy-start.35 = (f32[512,512]{1,0:T(8,128)S(1)}, f32[512,512]{1,0:T(8,128)}, u32[]{:S(2)}) copy-start(f32[512,512]{1,0:T(8,128)} %copy-done.34) | copy-start | bytes 3145732
  481.1 14.2 %copy-start.29 = (f32[512,512]{1,0:T(8,128)S(1)}, f32[512,512]{1,0:T(8,128)}, u32[]{:S(2)}) copy-start(f32[512,512]{1,0:T(8,128)} %get-tuple-element.160) | copy-start | bytes 3145732
  481.1 118.7 %reduce-scatter.9.cloned.1.call-start = ((), (), s32[]{:S(2)}) async-start(), calls=%async_computation.4 | async-start | bytes 1474560 | tf_op jit(solution)/shard_map/reduce_scatter | solution.py:959
  490.8 139.1 %reduce-scatter.11.cloned.1.call-start = ((), (), s32[]{:S(2)}) async-start(), calls=%async_computation.5 | async-start | bytes 1474560 | tf_op jit(solution)/shard_map/reduce_scatter | solution.py:959
  491.8 76.5 %collective-permute-start.6 = (f32[256,512]{1,0:T(8,128)}, f32[256,512]{1,0:T(8,128)S(1)}, u32[]{:S(2)}, u32[]{:S(2)}) collective-permute-start(f32[256,512]{1,0:T(8,128)} %get-tuple-element.156), channel_id=1, source_target_pairs={{0,0},{8,1},{2,2},{10,3},{4,4},{12,5},{6,6},{14,7},{16,8},{24,9},{... | collective-permute-start | bytes 1572872 | tf_op jit(solution)/shard_map/ppermute | solution.py:745
  493.5 74.8 %collective-permute-start.7 = (f32[256,512]{1,0:T(8,128)S(1)}, f32[256,512]{1,0:T(8,128)S(1)}, u32[]{:S(2)}, u32[]{:S(2)}) collective-permute-start(f32[256,512]{1,0:T(8,128)S(1)} %get-tuple-element.157), channel_id=1, source_target_pairs={{16,0},{24,1},{18,2},{26,3},{20,4},{28,5},{22,6},{30,7},{0,8},{8,9... | collective-permute-start | bytes 1572872 | tf_op jit(solution)/shard_map/ppermute | solution.py:745
  496.1 73.3 %collective-permute-start.15 = (f32[256,512]{1,0:T(8,128)}, f32[256,512]{1,0:T(8,128)S(1)}, u32[]{:S(2)}, u32[]{:S(2)}) collective-permute-start(f32[256,512]{1,0:T(8,128)} %get-tuple-element.148), channel_id=1, source_target_pairs={{0,0},{8,1},{2,2},{10,3},{4,4},{12,5},{6,6},{14,7},{16,8},{24,9},{... | collective-permute-start | bytes 1572872 | tf_op jit(solution)/shard_map/ppermute | solution.py:745
  497.8 71.6 %collective-permute-start.16 = (f32[256,512]{1,0:T(8,128)S(1)}, f32[256,512]{1,0:T(8,128)S(1)}, u32[]{:S(2)}, u32[]{:S(2)}) collective-permute-start(f32[256,512]{1,0:T(8,128)S(1)} %get-tuple-element.149), channel_id=1, source_target_pairs={{16,0},{24,1},{18,2},{26,3},{20,4},{28,5},{22,6},{30,7},{0,8},{8,9... | collective-permute-start | bytes 1572872 | tf_op jit(solution)/shard_map/ppermute | solution.py:745
  (71 other events, 172.0 us)
Sparse Core Ops, SparseCore 0:
  16.2 87.2 all-gather.4
  106.5 80.0 all-gather.6
  435.3 55.4 reduce-scatter.12
  493.6 74.5 reduce-scatter.14
  570.4 29.3 reduce-scatter.8
  602.0 27.9 reduce-scatter.10
